TPU v7x, 512 devices: a whole 4x8x8 slice. The times are simulated.
512 devices in a mesh: shard: 64 (over x, z, core), rep: 8 (over y).
Axes of the slice: x: 4, y: 8, z: 8, core: 2. Of those that a mesh axis runs over, the one named last changes fastest.
Arguments:
- attn_grad: bfloat16 [8, 2, 4, 768, 768], P('rep', None, None, 'shard'), may hold values from -16 to 16
- attn_error: float32 [8, 2, 4, 768, 768], P('rep', None, None, 'shard'), may hold values from -6 to 6
- attn_basis: float32 [2, 4, 768, 32], P(None, None, 'shard'), may hold values from -0.21875 to 0.21875
- attn_roots: float32 [2, 4, 3, 32, 32], replicated, as said below
- attn_momentum: float32 [2, 4, 768, 768], P(None, None, 'shard'), may hold values from -4 to 4
- attn_weights: float32 [2, 4, 768, 768], P(None, None, 'shard'), may hold values from -0.21875 to 0.21875
- mlp_grad: bfloat16 [8, 2, 2, 768, 3072], P('rep', None, None, 'shard'), may hold values from -16 to 16
- mlp_error: float32 [8, 2, 2, 768, 3072], P('rep', None, None, 'shard'), may hold values from -6 to 6
- mlp_basis: float32 [2, 2, 3072, 32], P(None, None, 'shard'), may hold values from -0.109375 to 0.109375
- mlp_roots: float32 [2, 2, 3, 32, 32], replicated, as said below
- mlp_momentum: float32 [2, 2, 768, 3072], P(None, None, 'shard'), may hold values from -4 to 4
- mlp_weights: float32 [2, 2, 768, 3072], P(None, None, 'shard'), may hold values from -0.21875 to 0.21875
- small_grad: bfloat16 [8, 2, 9984], P('rep', None, 'shard'), may hold values from -6 to 6
- small_momentum: float32 [2, 9984], P(None, 'shard'), may hold values from -4 to 4
- small_weights: float32 [2, 9984], P(None, 'shard'), may hold values from -6 to 6
Outputs:
- attn_error_out: float32 [8, 2, 4, 768, 768], P('rep', None, None, 'shard')
- mlp_error_out: float32 [8, 2, 2, 768, 3072], P('rep', None, None, 'shard')
- attn_left: float32 [2, 4, 768, 32], P(None, None, 'shard')
- attn_right: float32 [2, 4, 768, 32], P(None, None, 'shard')
- mlp_left: float32 [2, 2, 768, 32], P(None, None, 'shard')
- mlp_right: float32 [2, 2, 3072, 32], P(None, None, 'shard')
- attn_momentum_out: float32 [2, 4, 768, 768], P(None, None, 'shard')
- attn_weights_out: float32 [2, 4, 768, 768], P(None, None, 'shard')
- mlp_momentum_out: float32 [2, 2, 768, 3072], P(None, None, 'shard')
- mlp_weights_out: float32 [2, 2, 768, 3072], P(None, None, 'shard')
- small_momentum_out: float32 [2, 9984], P(None, 'shard')
- small_weights_out: float32 [2, 9984], P(None, 'shard')
Inputs may be any that keep to these rules, and one draw needn't show every extreme that they name: Every 32 x 32 factor of attn_roots is a scaled identity plus independent entries and is well conditioned. Every 32 x 32 factor of mlp_roots is a scaled identity plus independent entries and is well conditioned.
All inputs are finite; a program needn't handle non-finite values.
Results may differ from a plain program's by a relative error of at most 0.0003.
Values sent between devices are 32-bit elements; how exact they have to be, the bound alone decides.
A program may use at most 64 MiB of HBM per device.

v0:
```python
import jax
import jax.numpy as jnp
from jax import lax
from jax.sharding import PartitionSpec as P

momentum_decay = 0.9
learn_rate = 0.05


def rows_product(merged, factor):
    return jnp.einsum("lkrc,lkcn->lkrn", merged, factor, precision=lax.Precision.HIGHEST)


def cols_product(merged, factor):
    return jnp.einsum("lkrc,lkrn->lkcn", merged, factor, precision=lax.Precision.HIGHEST)


def rotate(factor, inverse_roots, round_index):
    return jnp.einsum(
        "lkrn,lknm->lkrm", factor, inverse_roots[:, :, round_index], precision=lax.Precision.HIGHEST
    )


def finish(summed, inverse_roots, round_index):
    if round_index < 0:
        return summed / float(lax.axis_size("rep"))
    return rotate(summed, inverse_roots, round_index)


def own_share(full_factor):
    share_width = full_factor.shape[2] // lax.axis_size("shard")
    share_start = lax.axis_index("shard") * share_width
    return lax.dynamic_slice_in_dim(full_factor, share_start, share_width, 2)


def column_round(attn_term, mlp_term, attn_roots, mlp_roots, round_index):
    attn_full, mlp_full = lax.psum((attn_term, mlp_term), ("shard", "rep"))
    attn_full = finish(attn_full, attn_roots, round_index)
    mlp_full = finish(mlp_full, mlp_roots, round_index)
    attn_share = own_share(attn_full)
    mlp_share = own_share(mlp_full)
    attn_next, mlp_next = (attn_full, mlp_full)
    return (attn_next, mlp_next, attn_full, mlp_full, attn_share, mlp_share)


def update(merged, approx, momentum, weights):
    error_out = (merged - approx)[None]
    momentum_out = momentum_decay * momentum + approx
    weights_out = weights - learn_rate * momentum_out
    return (error_out, momentum_out, weights_out)


def per_device(
    attn_grad,
    attn_error,
    attn_basis,
    attn_roots,
    attn_momentum,
    attn_weights,
    mlp_grad,
    mlp_error,
    mlp_basis,
    mlp_roots,
    mlp_momentum,
    mlp_weights,
    small_grad,
    small_momentum,
    small_weights,
):
    attn_merged = attn_grad[0].astype(jnp.float32) + attn_error[0]
    mlp_merged = mlp_grad[0].astype(jnp.float32) + mlp_error[0]
    small_local = small_grad[0].astype(jnp.float32)
    attn_bfull, mlp_bfull = (
        lax.all_gather(attn_basis, "shard", axis=2, tiled=True),
        lax.all_gather(mlp_basis, "shard", axis=2, tiled=True),
    )
    attn_data, mlp_data = (attn_merged, mlp_merged)
    attn_start, mlp_start = (attn_bfull, mlp_bfull)
    attn_first = rows_product(attn_data, attn_start)
    mlp_first = rows_product(mlp_data, mlp_start)
    small_total = lax.psum(small_local, "rep")
    attn_first, mlp_first = lax.psum((attn_first, mlp_first), "rep")
    attn_lhat = rotate(attn_first, attn_roots, 0)
    mlp_lhat = rotate(mlp_first, mlp_roots, 0)
    attn_rhat, mlp_rhat, spare_one, spare_two, spare_three, spare_four = column_round(
        cols_product(attn_data, attn_lhat),
        cols_product(mlp_data, mlp_lhat),
        attn_roots,
        mlp_roots,
        1,
    )
    attn_second, mlp_second = lax.psum(
        (rows_product(attn_data, attn_rhat), rows_product(mlp_data, mlp_rhat)), "rep"
    )
    attn_left = rotate(attn_second, attn_roots, 2)
    mlp_left = rotate(mlp_second, mlp_roots, 2)
    spare_five, spare_six, attn_rfull, mlp_rfull, attn_right, mlp_right = column_round(
        cols_product(attn_data, attn_left),
        cols_product(mlp_data, mlp_left),
        attn_roots,
        mlp_roots,
        -1,
    )
    attn_approx = jnp.einsum(
        "lkrn,lkcn->lkrc", attn_left, attn_rfull, precision=lax.Precision.HIGHEST
    )
    mlp_approx = jnp.einsum("lkrn,lkcn->lkrc", mlp_left, mlp_rfull, precision=lax.Precision.HIGHEST)
    attn_error_out, attn_momentum_out, attn_weights_out = update(
        attn_merged, attn_approx, attn_momentum, attn_weights
    )
    mlp_error_out, mlp_momentum_out, mlp_weights_out = update(
        mlp_merged, mlp_approx, mlp_momentum, mlp_weights
    )
    small_mean = small_total / float(lax.axis_size("rep"))
    small_momentum_out = momentum_decay * small_momentum + small_mean
    small_weights_out = small_weights - learn_rate * small_momentum_out
    return (
        attn_error_out,
        mlp_error_out,
        attn_left,
        attn_right,
        mlp_left,
        mlp_right,
        attn_momentum_out,
        attn_weights_out,
        mlp_momentum_out,
        mlp_weights_out,
        small_momentum_out,
        small_weights_out,
    )


def solution(mesh):
    in_specs = (
        P("rep", None, None, "shard", None),
        P("rep", None, None, "shard", None),
        P(None, None, "shard", None),
        P(),
        P(None, None, "shard", None),
        P(None, None, "shard", None),
        P("rep", None, None, "shard", None),
        P("rep", None, None, "shard", None),
        P(None, None, "shard", None),
        P(),
        P(None, None, "shard", None),
        P(None, None, "shard", None),
        P("rep", None, "shard"),
        P(None, "shard"),
        P(None, "shard"),
    )
    out_specs = (
        P("rep", None, None, "shard", None),
        P("rep", None, None, "shard", None),
        P(None, None, "shard", None),
        P(None, None, "shard", None),
        P(None, None, "shard", None),
        P(None, None, "shard", None),
        P(None, None, "shard", None),
        P(None, None, "shard", None),
        P(None, None, "shard", None),
        P(None, None, "shard", None),
        P(None, "shard"),
        P(None, "shard"),
    )
    return jax.shard_map(
        per_device, mesh=mesh, in_specs=in_specs, out_specs=out_specs, check_vma=False
    )
```

profile of v0, /device:TPU:1, one launch (start us, length us, event | category | flops | bytes accessed | tf_op | source)
XLA Modules:
  0.0 757.0 jit_solution(16800400785792100691)
XLA Ops:
  7.2 0.0 all-gather.2.cloned.1.call-start
  7.2 1.6 copy.101
  8.8 0.0 all-gather.2.cloned.1.call-update
  8.8 0.0 all-reduce.9.cloned.1.call-start
  8.9 0.8 copy.94
  9.7 0.0 copy-start.2
  9.7 0.0 copy-start.3
  9.7 59.7 %all_gather.6 = f32[2,4,768,32]{3,1,0,2:T(4,128)S(1)} all-gather(f32[2,4,12,32]{3,1,0,2:T(4,128)S(1)} %copy.94), channel_id=1, replica_groups=mesh['shard'=64,'rep'=8] {'shard'}, dimensions={2}, use_global_device_ids=true | all-gather | bytes 798720 | tf_op jit(solution)/shard_map/all_gather | solution.py:74
  69.4 0.0 copy-done.2
  69.4 0.0 copy-done.3
  69.4 0.0 copy-start
  69.4 0.0 copy-start.1
  69.4 2.1 fusion.2
  71.5 0.0 copy-start.11
  71.6 33.6 %all-gather.2.cloned.1.call-done = f32[2,2,3072,32]{3,1,0,2:T(2,128)} async-done(((f32[2,2,48,32]{3,1,0,2:T(2,128)}), f32[2,2,3072,32]{3,1,0,2:T(2,128)}) %all-gather.2.cloned.1.call-update) | async-done | bytes 1572880 | tf_op jit(solution)/shard_map/all_gather | solution.py:75
  105.2 0.0 copy-done
  105.2 0.0 copy-done.1
  105.2 6.1 fusion
  111.3 0.0 copy-start.12
  111.3 23.7 %all-reduce.3 = (f32[2,4,12,32]{3,2,1,0:T(8,128)S(1)}, f32[2,2,12,32]{3,2,1,0:T(8,128)S(1)}) all-reduce(f32[2,4,12,32]{3,2,1,0:T(8,128)S(1)} %fusion.2, f32[2,2,12,32]{3,2,1,0:T(8,128)S(1)} %fusion), channel_id=1, replica_groups=mesh['shard'=64,'rep'=8] {'rep'}, use_global_device_ids=true, to_apply=%region_0.0 | all-reduce | flops 4608 | bytes 36864 | tf_op jit(solution)/shard_map/psum | solution.py:82
  135.1 0.0 copy-done.11
  135.1 0.2 fusion.26
  135.3 1.7 fusion.17
  137.0 0.0 copy-done.12
  137.0 0.2 fusion.35
  137.2 2.8 fusion.8
  140.0 0.0 all-reduce.9.cloned.1.call-update
  140.0 0.2 all-reduce.7.cloned.1.call-start
  140.3 0.4 copy-done.15
  140.7 279.9 %all-reduce.9.cloned.1.call-done = (f32[2,4,768,32]{2,3,1,0:T(8,128)}, f32[2,2,3072,32]{2,3,1,0:T(8,128)}) async-done(((f32[2,4,768,32]{2,3,1,0:T(8,128)}, f32[2,2,3072,32]{2,3,1,0:T(8,128)}), (f32[2,4,768,32]{2,3,1,0:T(8,128)}, f32[2,2,3072,32]{2,3,1,0:T(8,128)})) %all-reduce.9.cloned.1.call-update) | async-done | bytes 2359312 | tf_op jit(solution)/shard_map/psum | solution.py:37
  420.6 2.1 fusion.22
  422.7 0.8 fusion.15
  423.5 1.5 fusion.31
  424.9 1.6 fusion.6
  426.6 23.4 %all-reduce.2 = (f32[2,4,12,32]{3,2,1,0:T(8,128)S(1)}, f32[2,2,12,32]{3,2,1,0:T(8,128)S(1)}, f32[2,156]{1,0:T(2,128)S(1)}) all-reduce(f32[2,4,12,32]{3,2,1,0:T(8,128)S(1)} %fusion.15, f32[2,2,12,32]{3,2,1,0:T(8,128)S(1)} %fusion.6, f32[2,156]{1,0:T(2,128)S(1)} %bitcast_convert_fusion), channel_id=1, replica_groups=mesh['shard'=64,'rep'=8] {'rep'}, use_global_device_ids=true, to_apply=%region_2.0 | all-reduce | flops 4920 | bytes 39360 | tf_op jit(solution)/shard_map/psum | solution.py:92
  450.0 0.2 fusion.24
  450.2 0.2 fusion.33
  450.4 1.7 fusion.13
  452.1 2.8 fusion.4
  454.9 0.0 all-reduce.7.cloned.1.call-update
  454.9 0.0 copy-start.9
  454.9 0.0 copy-start.10
  454.9 0.6 copy.114
  455.6 0.6 copy.112
  456.2 0.0 copy-done.14
  456.2 0.6 multiply_subtract_fusion
  456.8 280.8 %all-reduce.7.cloned.1.call-done = (f32[2,4,768,32]{2,3,1,0:T(8,128)}, f32[2,2,3072,32]{2,3,1,0:T(8,128)}) async-done(((f32[2,4,768,32]{2,3,1,0:T(8,128)}, f32[2,2,3072,32]{2,3,1,0:T(8,128)}), (f32[2,4,768,32]{2,3,1,0:T(8,128)}, f32[2,2,3072,32]{2,3,1,0:T(8,128)})) %all-reduce.7.cloned.1.call-update) | async-done | bytes 2359312 | tf_op jit(solution)/shard_map/psum | solution.py:37
  737.6 1.3 broadcast_multiply_fusion.1
  738.9 0.1 constant_dynamic-slice_fusion.1
  739.0 0.7 copy.113
  739.7 0.0 copy-done.9
  739.7 0.0 copy-done.5
  739.7 0.7 copy_subtract_fusion.1
  740.4 0.9 copy.116
  741.3 0.9 copy.115
  742.2 0.9 copy.110
  743.1 0.1 broadcast_multiply_fusion
  743.3 0.9 copy-done.7
  744.2 0.2 copy-done.8
  744.4 1.5 copy_subtract_fusion
  745.9 1.3 copy.118
  747.2 1.3 copy.117
  748.5 1.3 copy.111
  749.7 0.7 constant_dynamic-slice_fusion
  (13 shorter events, 0.0 us)
Async XLA Ops:
  7.2 98.0 %all-gather.2.cloned.1.call-start = ((), (), s32[]{:S(2)}) async-start(), calls=%async_computation | async-start | bytes 6389760 | tf_op jit(solution)/shard_map/all_gather | solution.py:75
  8.8 411.8 %all-reduce.9.cloned.1.call-start = ((), (), s32[]{:S(2)}) async-start(), calls=%async_computation.2 | async-start | bytes 4718592 | tf_op jit(solution)/shard_map/psum | solution.py:37
  9.7 59.7 %copy-start.2 = (f32[1,2,4,12,768]{4,2,3,1,0:T(4,128)S(1)}, f32[1,2,4,12,768]{4,2,3,1,0:T(4,128)}, u32[]{:S(2)}) copy-start(f32[1,2,4,12,768]{4,2,3,1,0:T(4,128)} %param.16) | copy-start | bytes 884740
  9.7 59.7 %copy-start.3 = (bf16[1,2,4,12,768]{4,2,3,1,0:T(4,128)(2,1)S(1)}, bf16[1,2,4,12,768]{4,2,3,1,0:T(4,128)(2,1)}, u32[]{:S(2)}) copy-start(bf16[1,2,4,12,768]{4,2,3,1,0:T(4,128)(2,1)} %param.15) | copy-start | bytes 442372
  69.4 35.8 %copy-start = (f32[1,2,2,12,3072]{4,2,3,1,0:T(2,128)S(1)}, f32[1,2,2,12,3072]{4,2,3,1,0:T(2,128)}, u32[]{:S(2)}) copy-start(f32[1,2,2,12,3072]{4,2,3,1,0:T(2,128)} %param.22) | copy-start | bytes 1769476
  69.4 35.8 %copy-start.1 = (bf16[1,2,2,12,3072]{4,2,3,1,0:T(2,128)(2,1)S(1)}, bf16[1,2,2,12,3072]{4,2,3,1,0:T(2,128)(2,1)}, u32[]{:S(2)}) copy-start(bf16[1,2,2,12,3072]{4,2,3,1,0:T(2,128)(2,1)} %param.21) | copy-start | bytes 884740
  71.5 63.5 %copy-start.11 = (f32[2,4,3,32,32]{4,3,2,1,0:T(8,128)S(1)}, f32[2,4,3,32,32]{4,3,2,1,0:T(8,128)}, u32[]{:S(2)}) copy-start(f32[2,4,3,32,32]{4,3,2,1,0:T(8,128)} %param.18) | copy-start | bytes 294916
  111.3 25.7 %copy-start.12 = (f32[2,2,3,32,32]{4,3,2,1,0:T(8,128)S(1)}, f32[2,2,3,32,32]{4,3,2,1,0:T(8,128)}, u32[]{:S(2)}) copy-start(f32[2,2,3,32,32]{4,3,2,1,0:T(8,128)} %param.24) | copy-start | bytes 147460
  140.0 0.7 copy-start.15
  140.0 597.6 %all-reduce.7.cloned.1.call-start = ((), (), s32[]{:S(2)}) async-start(), calls=%async_computation.1 | async-start | bytes 4718592 | tf_op jit(solution)/shard_map/psum | solution.py:37
  420.6 2.9 copy-start.6
  454.9 1.3 copy-start.13
  454.9 1.3 copy-start.14
  454.9 284.8 %copy-start.9 = (f32[2,4,12,768]{3,1,2,0:T(4,128)S(1)}, f32[2,4,12,768]{3,1,2,0:T(4,128)}, u32[]{:S(2)}) copy-start(f32[2,4,12,768]{3,1,2,0:T(4,128)} %param.20) | copy-start | bytes 884740
  454.9 284.8 %copy-start.10 = (f32[2,4,12,768]{3,1,2,0:T(4,128)S(1)}, f32[2,4,12,768]{3,1,2,0:T(4,128)}, u32[]{:S(2)}) copy-start(f32[2,4,12,768]{3,1,2,0:T(4,128)} %param.19) | copy-start | bytes 884740
  737.6 2.1 copy-start.5
  740.4 2.7 copy-start.4
  743.1 1.1 copy-start.7
  743.1 1.2 copy-start.8
Sparse Core Ops, SparseCore 0:
  11.9 93.1 all-gather.1
  140.1 280.3 all-reduce.8
  455.0 282.5 all-reduce.6
where the time goes:
time: 757 us
  waiting for transfers between devices  594 us (78%)
  blocking collectives  107 us (14%)
  matrix products  26.2 us (3%)
  between operations  14 us (2%)
  local copies, waits for them, and re-layouts  13.3 us (2%)
    psum x2, waiting for transfers between devices, column_round(): attn_full, mlp_full = lax.psum((attn_term, mlp_term), ('shard', 'rep'))  561 us
    all_gather x1, blocking collectives, per_device(): lax.all_gather(attn_basis, 'shard', axis=2, tiled=True)  59.7 us
    all_gather x1, waiting for transfers between devices, per_device(): lax.all_gather(mlp_basis, 'shard', axis=2, tiled=True)  33.6 us
    psum x1, blocking collectives, per_device(): attn_first, mlp_first = lax.psum((attn_first, mlp_first), 'rep')  23.7 us
    psum x1, blocking collectives, per_device(): lax.psum((rows_product(attn_data, attn_rhat), rows_product(mlp_data, mlp_...  23.4 us
  transfers between devices with their start and end apart: 3, of which 3 were waited for; matrix products, arithmetic and copies ran while one was open for 1% of the time, Pallas kernels for 0%

commit v1 on v0

v1 whole, which is shorter than its diff:
```python
import jax
import jax.numpy as jnp
from jax import lax
from jax.experimental import pallas as pl
from jax.experimental.pallas import tpu as pltpu
from jax.sharding import PartitionSpec as P

momentum_decay = 0.9
learn_rate = 0.05

MESH = pl.DeviceIdType.MESH
HI = lax.Precision.HIGHEST
LANES = 128
TILE = 8


def dot_nn(a, b):
    return lax.dot_general(
        a, b, (((1,), (0,)), ((), ())), precision=HI, preferred_element_type=jnp.float32
    )


def dot_nt(a, b):
    return lax.dot_general(
        a, b, (((1,), (1,)), ((), ())), precision=HI, preferred_element_type=jnp.float32
    )


def dot_tn(a, b):
    return lax.dot_general(
        a, b, (((0,), (0,)), ((), ())), precision=HI, preferred_element_type=jnp.float32
    )


def power_kernel(
    shape,
    x_ref,
    ba_ref,
    bm_ref,
    sg_ref,
    roots_ref,
    y_ref,
    small_ref,
    land_x,
    s_ref,
    land_ba,
    land_bm,
    basis_a,
    basis_m,
    land_sm,
    swap_out,
    swap_in,
    part,
    land_p,
    land_e,
    full,
    x_send,
    x_recv,
    sm_send,
    sm_recv,
    ba_send,
    ba_recv,
    bm_send,
    bm_recv,
    swap_send,
    swap_recv,
    p_send,
    p_recv,
    e_recv,
    g_send,
    ge_send,
    g_recv,
    y_send,
    y_recv,
):
    shards, reps, rows, cols_a, cols_m, rank, tiles = shape
    extra = tiles - shards
    half = shards // 2
    me = lax.axis_index("shard")
    rep = lax.axis_index("rep")
    side = lax.rem(rep, 2)
    pair = rep + 1 - 2 * side
    side_lo = side * half
    mine_in_side = jnp.logical_and(me >= side_lo, me < side_lo + half)

    def peer(step):
        return lax.rem(me + step, shards)

    def rep_peer(step):
        return lax.rem(rep + step, reps)

    def remote(src, dst, send, recv, where):
        return pltpu.make_async_remote_copy(
            src_ref=src,
            dst_ref=dst,
            send_sem=send,
            recv_sem=recv,
            device_id=where,
            device_id_type=MESH,
        )

    barrier = pltpu.get_barrier_semaphore()

    @pl.loop(1, reps)
    def _(step):
        pl.semaphore_signal(
            barrier, inc=1, device_id={"rep": rep_peer(step)}, device_id_type=MESH
        )

    @pl.loop(1, shards)
    def _(step):
        pl.semaphore_signal(barrier, inc=1, device_id={"shard": peer(step)}, device_id_type=MESH)

    pl.semaphore_wait(barrier, reps - 1 + shards - 1)

    def x_copy(step):
        to = rep_peer(step)
        return remote(
            x_ref.at[to], land_x.at[step], x_send.at[step], x_recv.at[step], {"rep": to}
        )

    def small_copy(step, slot):
        return remote(
            sg_ref, land_sm.at[slot], sm_send.at[step], sm_recv.at[slot], {"rep": rep_peer(step)}
        )

    def ba_copy(step, slot):
        return remote(
            ba_ref, land_ba.at[slot], ba_send.at[step], ba_recv.at[slot], {"shard": peer(step)}
        )

    def bm_copy(step, slot):
        return remote(
            bm_ref, land_bm.at[slot], bm_send.at[step], bm_recv.at[slot], {"shard": peer(step)}
        )

    @pl.loop(1, reps)
    def _(step):
        x_copy(step).start()

    @pl.loop(1, shards)
    def _(step):
        ba_copy(step, me).start()

    @pl.when(mine_in_side)
    def _():
        @pl.loop(1, shards)
        def _(step):
            bm_copy(step, me - side_lo).start()

        land_bm[me - side_lo] = bm_ref[...]

    @pl.loop(1, reps)
    def _(step):
        small_copy(step, rep).start()

    land_sm[rep] = sg_ref[...]
    land_ba[me] = ba_ref[...]

    @pl.loop(1, shards)
    def _(step):
        ba_copy(step, peer(step)).wait_recv()

    @pl.loop(0, half)
    def _(slot):
        @pl.when(slot + side_lo != me)
        def _():
            bm_copy(1, slot).wait_recv()

    @pl.loop(0, half)
    def _(slot):
        for core in range(2):
            basis_a[slot, core * rows : (core + 1) * rows, :] = land_ba[2 * slot + core]
        packed = land_bm[slot]
        for group in range(4):
            basis_m[slot, group * rows : (group + 1) * rows, :] = packed[
                :, group * rank : (group + 1) * rank
            ]

    s_ref[...] = jnp.zeros_like(s_ref)
    s_ref[0:rows, :] = x_ref[rep]

    @pl.loop(1, reps)
    def _(step):
        x_copy(step).wait_recv()
        s_ref[0:rows, :] += land_x[step]

    def swapped(turn, term):
        swap_out[turn] = term
        copy = remote(
            swap_out.at[turn],
            swap_in.at[turn],
            swap_send.at[turn],
            swap_recv.at[turn],
            {"rep": pair},
        )
        copy.start()
        copy.wait()
        return term + swap_in[turn]

    def right_round(turn, left_a, left_m, scale):
        mine = part.at[turn]
        right_a = dot_tn(left_a, s_ref[:, 0:cols_a])
        right_m = dot_tn(left_m, s_ref[:, cols_a : cols_a + cols_m])
        blocks_a = cols_a // LANES
        deep = rank // TILE
        for block in range((cols_a + cols_m) // LANES):
            if block < blocks_a:
                value = right_a[:, block * LANES : (block + 1) * LANES]
            else:
                at = block - blocks_a
                value = right_m[:, at * LANES : (at + 1) * LANES]
            part[turn, block * deep : (block + 1) * deep] = value.reshape(deep, TILE, LANES)

        def p_copy(step, slot):
            to = peer(step)
            return remote(
                mine.at[to],
                land_p.at[turn, slot],
                p_send.at[step],
                p_recv.at[turn, slot],
                {"shard": to},
            )

        def e_copy(owner, slot):
            return remote(
                mine.at[shards + owner],
                land_e.at[turn, slot],
                p_send.at[shards + owner],
                e_recv.at[turn, slot],
                {"shard": owner},
            )

        @pl.loop(0, extra)
        def _(owner):
            @pl.when(owner != me)
            def _():
                e_copy(owner, me).start()

        @pl.loop(1, shards)
        def _(step):
            p_copy(step, me).start()

        def g_copy(step, slot):
            return remote(
                full.at[turn, slot],
                full.at[turn, slot],
                g_send.at[step],
                g_recv.at[turn, slot],
                {"shard": peer(step)},
            )

        def ge_copy(step, slot):
            return remote(
                full.at[turn, shards + slot],
                full.at[turn, shards + slot],
                ge_send.at[step],
                g_recv.at[turn, shards + slot],
                {"shard": peer(step)},
            )

        @pl.when(me < extra)
        def _():
            land_e[turn, me] = part[turn, shards + me]

            @pl.loop(1, shards)
            def _(step):
                e_copy(0, peer(step)).wait_recv()

            full[turn, shards + me] = jnp.sum(land_e[turn], axis=0) * scale

            @pl.loop(1, shards)
            def _(step):
                ge_copy(step, me).start()

        land_p[turn, me] = part[turn, me]

        @pl.loop(1, shards)
        def _(step):
            p_copy(step, peer(step)).wait_recv()

        full[turn, me] = jnp.sum(land_p[turn], axis=0) * scale

        @pl.loop(1, shards)
        def _(step):
            g_copy(step, me).start()

        @pl.loop(0, extra)
        def _(owner):
            @pl.when(owner != me)
            def _():
                ge_copy(1, owner).wait_recv()

        @pl.loop(1, shards)
        def _(step):
            g_copy(step, peer(step)).wait_recv()

        @pl.loop(1, shards)
        def _(step):
            p_copy(step, me).wait_send()
            g_copy(step, me).wait_send()

        @pl.loop(0, extra)
        def _(owner):
            @pl.when(owner != me)
            def _():
                e_copy(owner, me).wait_send()

        @pl.when(me < extra)
        def _():
            @pl.loop(1, shards)
            def _(step):
                ge_copy(step, me).wait_send()

        pieces = [
            full[turn, block * deep : (block + 1) * deep].reshape(rank, LANES)
            for block in range((cols_a + cols_m) // LANES)
        ]
        return (
            jnp.concatenate(pieces[:blocks_a], axis=1),
            jnp.concatenate(pieces[blocks_a:], axis=1),
        )

    basis_full_a = basis_a[...].reshape(cols_a, rank)
    basis_full_m = basis_m[...].reshape(cols_m, rank)
    first_m = dot_nn(s_ref[:, cols_a : cols_a + cols_m], basis_full_m)
    first_a = dot_nn(s_ref[:, 0:cols_a], basis_full_a)
    first_m = swapped(0, first_m)
    lhat_a = dot_nn(first_a, roots_ref[0, 0])
    lhat_m = dot_nn(first_m, roots_ref[1, 0])
    one_a, one_m = right_round(0, lhat_a, lhat_m, 1.0)
    second_m = swapped(1, dot_nt(s_ref[:, cols_a : cols_a + cols_m], one_m))
    second_a = dot_nt(s_ref[:, 0:cols_a], one_a)
    left_a = dot_nn(dot_nn(second_a, roots_ref[0, 1]), roots_ref[0, 2])
    left_m = dot_nn(dot_nn(second_m, roots_ref[1, 1]), roots_ref[1, 2])
    right_a, right_m = right_round(1, left_a, left_m, 1.0 / reps)

    y_ref[rep, :, 0:cols_a] = dot_nn(left_a, right_a)[0:rows]
    y_ref[rep, :, cols_a : cols_a + cols_m] = dot_nn(left_m, right_m)[0:rows]
    padded = left_a.shape[0]
    line = lax.broadcasted_iota(jnp.int32, (padded, cols_a), 0)
    column = lax.broadcasted_iota(jnp.int32, (padded, cols_a), 1)
    pick_a = jnp.where(column == me * rows + line, 1.0, 0.0).astype(jnp.float32)
    line = lax.broadcasted_iota(jnp.int32, (padded, cols_m), 0)
    column = lax.broadcasted_iota(jnp.int32, (padded, cols_m), 1)
    factors = [left_a, left_m, dot_nt(pick_a, right_a)]
    for group in range(4):
        start = (me - side_lo) * (4 * rows) + group * rows
        pick_m = jnp.where(column == start + line, 1.0, 0.0).astype(jnp.float32)
        factors.append(dot_nt(pick_m, right_m))
    factors.append(jnp.zeros_like(left_a))
    for at, factor in enumerate(factors):
        lo = cols_a + cols_m + at * rank
        y_ref[rep, :, lo : lo + rank] = factor[0:rows]

    def y_copy(step, slot):
        return remote(
            y_ref.at[slot], y_ref.at[slot], y_send.at[step], y_recv.at[slot], {"rep": rep_peer(step)}
        )

    @pl.loop(1, reps)
    def _(step):
        y_copy(step, rep).start()

    @pl.loop(1, reps)
    def _(step):
        small_copy(step, rep_peer(step)).wait_recv()

    total = land_sm[0]
    for slot in range(1, reps):
        total = total + land_sm[slot]
    small_ref[...] = total

    @pl.loop(1, shards)
    def _(step):
        ba_copy(step, me).wait_send()

    @pl.when(mine_in_side)
    def _():
        @pl.loop(1, shards)
        def _(step):
            bm_copy(step, me - side_lo).wait_send()

    @pl.loop(1, reps)
    def _(step):
        x_copy(step).wait_send()
        small_copy(step, rep).wait_send()

    @pl.loop(1, reps)
    def _(step):
        y_copy(step, rep_peer(step)).wait_recv()
        y_copy(step, rep).wait_send()


def power_call(shape, x, ba, bm, sg, roots):
    shards, reps, rows, cols_a, cols_m, rank, tiles = shape
    padded = 16
    half = shards // 2
    width = cols_a + cols_m
    wide = width + 8 * rank
    f32 = jnp.float32
    vmem = pl.BlockSpec(memory_space=pltpu.VMEM)
    dma = pltpu.SemaphoreType.DMA

    def body(*refs):
        power_kernel(shape, *refs)

    return pl.pallas_call(
        body,
        out_shape=(
            jax.ShapeDtypeStruct((reps, rows, wide), f32),
            jax.ShapeDtypeStruct(sg.shape, f32),
        ),
        in_specs=[vmem] * 5,
        out_specs=(vmem, vmem),
        scratch_shapes=[
            pltpu.VMEM((reps, rows, width), f32),
            pltpu.VMEM((padded, width), f32),
            pltpu.VMEM((shards, rows, rank), f32),
            pltpu.VMEM((half, rows, 4 * rank), f32),
            pltpu.VMEM((half, 2 * rows, rank), f32),
            pltpu.VMEM((half, 4 * rows, rank), f32),
            pltpu.VMEM((reps,) + sg.shape, f32),
            pltpu.VMEM((2, padded, rank), f32),
            pltpu.VMEM((2, padded, rank), f32),
            pltpu.VMEM((2, tiles, TILE, LANES), f32),
            pltpu.VMEM((2, shards, TILE, LANES), f32),
            pltpu.VMEM((2, shards, TILE, LANES), f32),
            pltpu.VMEM((2, tiles, TILE, LANES), f32),
            dma((reps,)),
            dma((reps,)),
            dma((reps,)),
            dma((reps,)),
            dma((shards,)),
            dma((shards,)),
            dma((shards,)),
            dma((half,)),
            dma((2,)),
            dma((2,)),
            dma((tiles,)),
            dma((2, shards)),
            dma((2, shards)),
            dma((shards,)),
            dma((shards,)),
            dma((2, tiles)),
            dma((reps,)),
            dma((reps,)),
        ],
        compiler_params=pltpu.CompilerParams(collective_id=0, has_side_effects=True),
        name="power_rounds",
    )(x, ba, bm, sg, roots)


def update(merged, approx, momentum, weights):
    error_out = (merged - approx)[None]
    momentum_out = momentum_decay * momentum + approx
    weights_out = weights - learn_rate * momentum_out
    return (error_out, momentum_out, weights_out)


def pick(array, index):
    return lax.dynamic_index_in_dim(array, index, 0, keepdims=False)


def per_device(
    attn_grad,
    attn_error,
    attn_basis,
    attn_roots,
    attn_momentum,
    attn_weights,
    mlp_grad,
    mlp_error,
    mlp_basis,
    mlp_roots,
    mlp_momentum,
    mlp_weights,
    small_grad,
    small_momentum,
    small_weights,
):
    shards, reps = lax.axis_size("shard"), lax.axis_size("rep")
    layers, kinds_a, rows, cols_a = attn_error.shape[1:]
    kinds_m, _, columns_m = mlp_error.shape[2:]
    rank = attn_basis.shape[-1]
    mats_a, mats_m = layers * kinds_a, layers * kinds_m
    cols_m = columns_m // 2
    assert mats_a == reps and 2 * mats_m == reps
    rep = lax.axis_index("rep")

    attn_merged = attn_grad[0].astype(jnp.float32) + attn_error[0]
    mlp_merged = mlp_grad[0].astype(jnp.float32) + mlp_error[0]
    x = jnp.concatenate(
        [
            attn_merged.reshape(mats_a, rows, cols_a),
            mlp_merged.reshape(mats_m, rows, 2, cols_m)
            .transpose(0, 2, 1, 3)
            .reshape(reps, rows, cols_m),
        ],
        axis=2,
    )
    ba = pick(attn_basis.reshape(mats_a, rows, rank), rep)
    bm = pick(mlp_basis.reshape(mats_m, 4, rows, rank), rep // 2)
    bm = bm.transpose(1, 0, 2).reshape(rows, 4 * rank)
    roots = jnp.stack(
        [
            pick(attn_roots.reshape(mats_a, 3, rank, rank), rep),
            pick(mlp_roots.reshape(mats_m, 3, rank, rank), rep // 2),
        ]
    )
    entries = small_grad.shape[1] * small_grad.shape[2]
    lines = -(-entries // LANES)
    sg = small_grad[0].astype(jnp.float32).reshape(entries)
    sg = jnp.pad(sg, (0, lines * LANES - entries)).reshape(lines, LANES)
    tiles = (cols_a + cols_m) * rank // (TILE * LANES)

    y, small = power_call((shards, reps, rows, cols_a, cols_m, rank, tiles), x, ba, bm, sg, roots)

    attn_approx = y[:, :, :cols_a].reshape(layers, kinds_a, rows, cols_a)
    mlp_approx = (
        y[:, :, cols_a : cols_a + cols_m]
        .reshape(mats_m, 2, rows, cols_m)
        .transpose(0, 2, 1, 3)
        .reshape(layers, kinds_m, rows, columns_m)
    )
    factors = y[:, :, cols_a + cols_m :].reshape(reps, rows, 8, rank)
    attn_left = factors[:, :, 0].reshape(layers, kinds_a, rows, rank)
    mlp_left = factors[0::2, :, 1].reshape(layers, kinds_m, rows, rank)
    attn_right = factors[:, :, 2].reshape(layers, kinds_a, rows, rank)
    mlp_right = factors[0::2, :, 3:7] + factors[1::2, :, 3:7]
    mlp_right = mlp_right.transpose(0, 2, 1, 3).reshape(layers, kinds_m, 4 * rows, rank)

    attn_error_out, attn_momentum_out, attn_weights_out = update(
        attn_merged, attn_approx, attn_momentum, attn_weights
    )
    mlp_error_out, mlp_momentum_out, mlp_weights_out = update(
        mlp_merged, mlp_approx, mlp_momentum, mlp_weights
    )
    small_total = small.reshape(lines * LANES)[:entries].reshape(small_momentum.shape)
    small_mean = small_total / float(reps)
    small_momentum_out = momentum_decay * small_momentum + small_mean
    small_weights_out = small_weights - learn_rate * small_momentum_out
    return (
        attn_error_out,
        mlp_error_out,
        attn_left,
        attn_right,
        mlp_left,
        mlp_right,
        attn_momentum_out,
        attn_weights_out,
        mlp_momentum_out,
        mlp_weights_out,
        small_momentum_out,
        small_weights_out,
    )


def solution(mesh):
    in_specs = (
        P("rep", None, None, "shard", None),
        P("rep", None, None, "shard", None),
        P(None, None, "shard", None),
        P(),
        P(None, None, "shard", None),
        P(None, None, "shard", None),
        P("rep", None, None, "shard", None),
        P("rep", None, None, "shard", None),
        P(None, None, "shard", None),
        P(),
        P(None, None, "shard", None),
        P(None, None, "shard", None),
        P("rep", None, "shard"),
        P(None, "shard"),
        P(None, "shard"),
    )
    out_specs = (
        P("rep", None, None, "shard", None),
        P("rep", None, None, "shard", None),
        P(None, None, "shard", None),
        P(None, None, "shard", None),
        P(None, None, "shard", None),
        P(None, None, "shard", None),
        P(None, None, "shard", None),
        P(None, None, "shard", None),
        P(None, None, "shard", None),
        P(None, None, "shard", None),
        P(None, "shard"),
        P(None, "shard"),
    )
    return jax.shard_map(
        per_device, mesh=mesh, in_specs=in_specs, out_specs=out_specs, check_vma=False
    )
```

time: 757 us -> 165 us (0.22)
  waiting for transfers between devices: 594 us -> 0 us
  Pallas kernels: 0 us -> 141 us
  blocking collectives: 107 us -> 0 us
  matrix products: 26.2 us -> 0 us
  between operations: 14 us -> 0.9 us
    psum x2 -> x0, waiting for transfers between devices: 561 us -> none  [column_round(): attn_full, mlp_full = lax.psum((attn_term, mlp_term), ('shard', 'rep'))]
    pallas_call x0 -> x1, Pallas kernels: none -> 141 us  [power_call(): pl.pallas_call(body, out_shape=(jax.ShapeDtypeStruct((reps, rows, wide),...]
    all_gather x1 -> x0, blocking collectives: 59.7 us -> none  [per_device(): lax.all_gather(attn_basis, 'shard', axis=2, tiled=True)]
    psum x2 -> x0, blocking collectives: 47.1 us -> none  [the longest x1 23.7 us: per_device(): attn_first, mlp_first = lax.psum((attn_first, mlp_first), 'rep')]
    all_gather x1 -> x0, waiting for transfers between devices: 33.6 us -> none  [per_device(): lax.all_gather(mlp_basis, 'shard', axis=2, tiled=True)]
    dot_general x16 -> x0, matrix products: 26.2 us -> none  [the longest x4 10.7 us: rows_product(): jnp.einsum('lkrc,lkcn->lkrn', merged, factor, precision=lax.Precision.HIG...]
  transfers between devices with their start and end apart: 3 -> 0, of which waited for: 3 -> 0; matrix products, arithmetic and copies ran while one was open for 1% -> 0% of each run, Pallas kernels for 0% -> 0%
where the time goes in v1:
time: 165 us; the launch traced here: 164 us
  Pallas kernels  141 us (85%)
  local copies, waits for them, and re-layouts  14.4 us (9%)
  other arithmetic  8.24 us (5%)
    pallas_call x1, Pallas kernels, power_call(): pl.pallas_call(body, out_shape=(jax.ShapeDtypeStruct((reps, rows, wide),...  141 us
    unnamed x28, local copies, waits for them, and re-layouts  7.61 us

profile of v1, /device:TPU:1, one launch (start us, length us, event | category | flops | bytes accessed | tf_op | source)
XLA Modules:
  0.0 164.4 jit_solution(2174545012390128265)
XLA Ops:
  0.6 0.0 copy-start.1
  0.7 0.0 copy-start.4
  0.7 0.8 convert_element_type.21
  1.5 0.6 bitcast_convert_fusion.refs_3_
  2.1 0.8 copy.56
  2.9 0.6 copy.89
  3.5 0.8 constant_dynamic-slice_fusion
  4.4 0.6 pad_maximum_fusion.1.refs_4_
  5.0 1.0 copy.57
  6.0 0.7 reshape.91.refs_2_
  6.7 1.0 convert_add_fusion
  7.7 0.1 copy.52
  7.8 0.0 copy-done.1
  7.8 0.0 copy-done.4
  7.8 0.3 copy_add_fusion
  8.2 0.7 add.46
  8.9 0.4 copy.55
  9.2 1.1 pad_maximum_fusion.refs_0_
  10.4 0.0 copy-start.7
  10.4 0.0 copy-start.8
  10.4 140.9 %power_rounds.1 = (f32[8,12,2560]{2,1,0:T(8,128)}, f32[3,128]{1,0:T(4,128)}) custom-call(f32[8,12,2304]{2,1,0:T(8,128)} %pad_maximum_fusion.refs_0_, f32[12,32]{1,0:T(8,128)} %bitcast.61, f32[12,128]{1,0:T(8,128)} %reshape.91.refs_2_, f32[3,128]{1,0:T(4,128)} %bitcast_convert_fusion.refs_3_, f32[2,3,32,32]{3,2,1,0:T(8,128)} %pad_maximum_fusion.1.refs_4_), custom_call_target="tpu_custom_call" | custom-call | tf_op jit(solution)/shard_map/power_rounds/pallas_call | solution.py:408
  151.3 0.0 copy-start
  151.3 0.8 slice_multiply_fusion
  152.0 0.1 div.22
  152.1 0.0 copy-done.7
  152.1 0.0 copy-done.8
  152.1 0.6 multiply_subtract_fusion.1
  152.7 0.9 slice.29
  153.6 0.1 copy.61
  153.7 0.1 reshape.99
  153.9 0.6 copy.69
  154.5 0.1 fusion.2
  154.6 0.6 copy.68
  155.2 0.6 copy.67
  155.9 0.7 copy.70
  156.6 0.0 copy-done
  156.7 0.1 slice.28
  156.7 0.5 copy.87
  157.2 0.9 copy_subtract_fusion.1
  158.1 0.7 reshape.102
  158.8 0.7 reshape.98
  159.6 0.0 copy-start.2
  159.6 0.0 copy-start.3
  159.6 0.3 sub.24
  159.9 0.9 copy.66
  160.8 0.0 copy-done.2
  160.8 0.0 copy-done.3
  160.8 0.7 copy_subtract_fusion
  161.5 0.0 copy-start.5
  161.5 0.0 copy-start.6
  161.5 0.9 copy.72
  162.4 0.9 copy.71
  163.2 0.0 copy-done.5
  163.2 0.0 copy-done.6
  163.3 1.2 multiply_subtract_fusion
  (7 shorter events, 0.2 us)
Async XLA Ops:
  0.6 7.2 %copy-start.1 = (f32[1,2,2,12,3072]{4,2,3,1,0:T(2,128)S(1)}, f32[1,2,2,12,3072]{4,2,3,1,0:T(2,128)}, u32[]{:S(2)}) copy-start(f32[1,2,2,12,3072]{4,2,3,1,0:T(2,128)} %param.22) | copy-start | bytes 1769476
  0.7 7.2 %copy-start.4 = (bf16[1,2,2,12,3072]{4,2,3,1,0:T(2,128)(2,1)S(1)}, bf16[1,2,2,12,3072]{4,2,3,1,0:T(2,128)(2,1)}, u32[]{:S(2)}) copy-start(bf16[1,2,2,12,3072]{4,2,3,1,0:T(2,128)(2,1)} %param.21) | copy-start | bytes 884740
  10.4 141.8 %copy-start.7 = (f32[2,156]{1,0:T(2,128)S(1)}, f32[2,156]{1,0:T(2,128)}, u32[]{:S(2)}) copy-start(f32[2,156]{1,0:T(2,128)} %param.29) | copy-start | bytes 3748
  10.4 141.8 %copy-start.8 = (f32[2,156]{1,0:T(2,128)S(1)}, f32[2,156]{1,0:T(2,128)}, u32[]{:S(2)}) copy-start(f32[2,156]{1,0:T(2,128)} %param.28) | copy-start | bytes 3748
  151.3 5.4 %copy-start = (f32[8,12,2560]{2,1,0:T(8,128)S(1)}, f32[8,12,2560]{2,1,0:T(8,128)}, u32[]{:S(2)}) copy-start(f32[8,12,2560]{2,1,0:T(8,128)} %get-tuple-element.14) | copy-start | bytes 2949124
  159.6 1.2 copy-start.2
  159.6 1.2 copy-start.3
  161.5 1.7 %copy-start.5 = (f32[2,4,12,768]{3,1,2,0:T(4,128)S(1)}, f32[2,4,12,768]{3,1,2,0:T(4,128)}, u32[]{:S(2)}) copy-start(f32[2,4,12,768]{3,1,2,0:T(4,128)} %param.20) | copy-start | bytes 884740
  161.5 1.7 %copy-start.6 = (f32[2,4,12,768]{3,1,2,0:T(4,128)S(1)}, f32[2,4,12,768]{3,1,2,0:T(4,128)}, u32[]{:S(2)}) copy-start(f32[2,4,12,768]{3,1,2,0:T(4,128)} %param.19) | copy-start | bytes 884740

commit v2 on v1

v2 whole, which is shorter than its diff:
```python
import jax
import jax.numpy as jnp
from jax import lax
from jax.experimental import pallas as pl
from jax.experimental.pallas import tpu as pltpu
from jax.sharding import PartitionSpec as P

momentum_decay = 0.9
learn_rate = 0.05

MESH = pl.DeviceIdType.MESH
HI = lax.Precision.HIGHEST
LANES = 128
TILE = 8


def dot_nn(a, b):
    return lax.dot_general(
        a, b, (((1,), (0,)), ((), ())), precision=HI, preferred_element_type=jnp.float32
    )


def dot_nt(a, b):
    return lax.dot_general(
        a, b, (((1,), (1,)), ((), ())), precision=HI, preferred_element_type=jnp.float32
    )


def dot_tn(a, b):
    return lax.dot_general(
        a, b, (((0,), (0,)), ((), ())), precision=HI, preferred_element_type=jnp.float32
    )


GROUP = 8
PIECES = 3


def power_kernel(
    shape,
    x_ref,
    ba_ref,
    bm_ref,
    sg_ref,
    roots_ref,
    y_ref,
    small_ref,
    land_x,
    sum_x,
    s_ref,
    land_ba,
    land_bm,
    basis_a,
    basis_m,
    land_sm,
    swap_out,
    swap_in,
    part,
    land_p,
    part_z,
    land_z,
    full,
    x_send,
    x_recv,
    y_send,
    y_recv,
    sm_send,
    sm_recv,
    b_send,
    b_recv,
    c_send,
    c_recv,
    swap_send,
    swap_recv,
    p_send,
    p_recv,
    z_send,
    z_recv,
    g_send,
    g_recv,
):
    shards, reps, rows, cols_a, cols_m, rank, tiles = shape
    width = cols_a + cols_m
    wide = y_ref.shape[2]
    me = lax.axis_index("shard")
    rep = lax.axis_index("rep")
    side = lax.rem(rep, 2)
    pair = rep + 1 - 2 * side
    core = lax.rem(me, 2)
    deep = lax.rem(me // 2, GROUP)
    flat = (me // (2 * GROUP)) * 2 + core
    way = 1 - 2 * core
    in_side = flat // 4 == side
    near = flat - 4 * side

    def flat_peer(step):
        to = lax.rem(flat + step, GROUP)
        return to, {"shard": (to // 2) * (2 * GROUP) + deep * 2 + lax.rem(to, 2)}

    def deep_peer(step):
        to = lax.rem(deep + step, GROUP)
        return to, {"shard": (flat // 2) * (2 * GROUP) + to * 2 + core}

    def rep_at(offset):
        return lax.rem(rep + offset + 2 * reps, reps)

    def remote(src, dst, send, recv, where):
        return pltpu.make_async_remote_copy(
            src_ref=src,
            dst_ref=dst,
            send_sem=send,
            recv_sem=recv,
            device_id=where,
            device_id_type=MESH,
        )

    barrier = pltpu.get_barrier_semaphore()

    def greet(where):
        pl.semaphore_signal(barrier, inc=1, device_id=where, device_id_type=MESH)

    @pl.loop(1, reps)
    def _(step):
        greet({"rep": rep_at(step)})

    @pl.loop(1, GROUP)
    def _(step):
        greet(flat_peer(step)[1])
        greet(deep_peer(step)[1])

    pl.semaphore_wait(barrier, reps - 1 + 2 * (GROUP - 1))

    def cuts(total):
        count = total // LANES
        share = -(-count // PIECES)
        edges = [min(at * share, count) * LANES for at in range(PIECES + 1)]
        return [slice(lo, hi) for lo, hi in zip(edges[:-1], edges[1:])]

    turns = ((0, 4), (1, 3))

    def x_copy(route, step, piece):
        steps = turns[route][1]
        sign = way if route == 0 else -way
        cut = cuts(width)[piece]
        slot = 4 * route + step
        if step == 0:
            source = x_ref.at[rep_at(steps * sign), :, cut]
        else:
            source = sum_x.at[slot, :, cut]
        return remote(
            source,
            land_x.at[slot, :, cut],
            x_send.at[slot, piece],
            x_recv.at[slot, piece],
            {"rep": rep_at(sign)},
        )

    for piece in range(PIECES):
        for route, _ in turns:
            x_copy(route, 0, piece).start()

    def ba_first(step, slot):
        to, where = flat_peer(step)
        return remote(
            ba_ref, land_ba.at[deep, slot], b_send.at[0, step], b_recv.at[0, slot], where
        )

    def bm_first(step, slot):
        to, where = flat_peer(step)
        return remote(
            bm_ref, land_bm.at[deep, slot], b_send.at[1, step], b_recv.at[1, slot], where
        )

    def ba_second(step, slot):
        to, where = deep_peer(step)
        return remote(
            land_ba.at[slot], land_ba.at[slot], c_send.at[0, step], c_recv.at[0, slot], where
        )

    def bm_second(step, slot):
        to, where = deep_peer(step)
        return remote(
            land_bm.at[slot], land_bm.at[slot], c_send.at[1, step], c_recv.at[1, slot], where
        )

    def small_copy(step, slot):
        return remote(
            sg_ref, land_sm.at[slot], sm_send.at[step], sm_recv.at[slot], {"rep": rep_at(step)}
        )

    @pl.loop(1, GROUP)
    def _(step):
        ba_first(step, flat).start()

    land_ba[deep, flat] = ba_ref[...]

    @pl.when(in_side)
    def _():
        @pl.loop(1, GROUP)
        def _(step):
            bm_first(step, near).start()

        land_bm[deep, near] = bm_ref[...]

    @pl.loop(1, reps)
    def _(step):
        small_copy(step, rep).start()

    land_sm[rep] = sg_ref[...]

    @pl.loop(1, GROUP)
    def _(step):
        ba_first(step, flat_peer(step)[0]).wait_recv()

    @pl.loop(0, 4)
    def _(slot):
        @pl.when(slot != near)
        def _():
            bm_first(1, slot).wait_recv()

    @pl.loop(1, GROUP)
    def _(step):
        ba_second(step, deep).start()
        bm_second(step, deep).start()

    for step in range(1, 4):
        for piece in range(PIECES):
            for route, steps in turns:
                if step < steps:
                    sign = way if route == 0 else -way
                    cut = cuts(width)[piece]
                    x_copy(route, step - 1, piece).wait_recv()
                    sum_x[4 * route + step, :, cut] = (
                        land_x[4 * route + step - 1, :, cut]
                        + x_ref[rep_at((steps - step) * sign), :, cut]
                    )
                    x_copy(route, step, piece).start()

    @pl.loop(1, GROUP)
    def _(step):
        ba_second(step, deep_peer(step)[0]).wait_recv()
        bm_second(step, deep_peer(step)[0]).wait_recv()

    @pl.loop(0, GROUP)
    def _(slot):
        for place in range(GROUP):
            lo = (place % 2) * rows
            basis_a[(place // 2) * GROUP + slot, lo : lo + rows, :] = land_ba[slot, place]
        for place in range(4):
            packed = land_bm[slot, place]
            for group in range(4):
                basis_m[
                    ((place // 2) * GROUP + slot) * 2 + place % 2,
                    group * rows : (group + 1) * rows,
                    :,
                ] = packed[:, group * rank : (group + 1) * rank]

    s_ref[...] = jnp.zeros_like(s_ref)
    for piece in range(PIECES):
        cut = cuts(width)[piece]
        for route, steps in turns:
            x_copy(route, steps - 1, piece).wait_recv()
        s_ref[0:rows, cut] = x_ref[rep, :, cut] + (land_x[3, :, cut] + land_x[6, :, cut])

    def swapped(turn, term):
        swap_out[turn] = term
        copy = remote(
            swap_out.at[turn],
            swap_in.at[turn],
            swap_send.at[turn],
            swap_recv.at[turn],
            {"rep": pair},
        )
        copy.start()
        copy.wait()
        return term + swap_in[turn]

    share = tiles // GROUP
    blocks_a, blocks = cols_a // LANES, width // LANES
    high = rank // TILE

    def right_round(turn, left_a, left_m, scale):
        right_a = dot_tn(left_a, s_ref[:, 0:cols_a])
        right_m = dot_tn(left_m, s_ref[:, cols_a:width])
        for block in range(blocks):
            value, at = (right_a, block) if block < blocks_a else (right_m, block - blocks_a)
            for line in range(high):
                tile = block * high + line
                part[turn, tile // share, tile % share] = value[
                    line * TILE : (line + 1) * TILE, at * LANES : (at + 1) * LANES
                ]

        def p_copy(step, slot):
            to, where = flat_peer(step)
            return remote(
                part.at[turn, to],
                land_p.at[turn, slot],
                p_send.at[turn, step],
                p_recv.at[turn, slot],
                where,
            )

        def z_copy(step, slot):
            to, where = deep_peer(step)
            return remote(
                part_z.at[turn],
                land_z.at[turn, slot],
                z_send.at[turn, step],
                z_recv.at[turn, slot],
                where,
            )

        def g_copy(step, slot):
            to, where = flat_peer(step)
            return remote(
                full.at[turn, slot],
                full.at[turn, slot],
                g_send.at[turn, step],
                g_recv.at[turn, slot],
                where,
            )

        @pl.loop(1, GROUP)
        def _(step):
            p_copy(step, flat).start()

        land_p[turn, flat] = part[turn, flat]

        @pl.loop(1, GROUP)
        def _(step):
            p_copy(step, flat_peer(step)[0]).wait_recv()

        part_z[turn] = jnp.sum(land_p[turn], axis=0)

        @pl.loop(1, GROUP)
        def _(step):
            z_copy(step, deep).start()

        land_z[turn, deep] = part_z[turn]

        @pl.loop(1, GROUP)
        def _(step):
            z_copy(step, deep_peer(step)[0]).wait_recv()

        full[turn, flat] = jnp.sum(land_z[turn], axis=0) * scale

        @pl.loop(1, GROUP)
        def _(step):
            g_copy(step, flat).start()

        @pl.loop(1, GROUP)
        def _(step):
            g_copy(step, flat_peer(step)[0]).wait_recv()

        @pl.loop(1, GROUP)
        def _(step):
            p_copy(step, flat).wait_send()
            z_copy(step, deep).wait_send()
            g_copy(step, flat).wait_send()

        whole = full[turn].reshape(tiles, TILE, LANES)
        pieces = [
            whole[block * high : (block + 1) * high].reshape(rank, LANES) for block in range(blocks)
        ]
        return (
            jnp.concatenate(pieces[:blocks_a], axis=1),
            jnp.concatenate(pieces[blocks_a:], axis=1),
        )

    basis_full_a = basis_a[...].reshape(cols_a, rank)
    basis_full_m = basis_m[...].reshape(cols_m, rank)
    first_m = dot_nn(s_ref[:, cols_a:width], basis_full_m)
    first_a = dot_nn(s_ref[:, 0:cols_a], basis_full_a)
    first_m = swapped(0, first_m)
    lhat_a = dot_nn(first_a, roots_ref[0, 0])
    lhat_m = dot_nn(first_m, roots_ref[1, 0])
    one_a, one_m = right_round(0, lhat_a, lhat_m, 1.0)
    second_m = swapped(1, dot_nt(s_ref[:, cols_a:width], one_m))
    second_a = dot_nt(s_ref[:, 0:cols_a], one_a)
    left_a = dot_nn(dot_nn(second_a, roots_ref[0, 1]), roots_ref[0, 2])
    left_m = dot_nn(dot_nn(second_m, roots_ref[1, 1]), roots_ref[1, 2])
    right_a, right_m = right_round(1, left_a, left_m, 1.0 / reps)

    def y_copy(route, step, piece):
        sign = way if route == 0 else -way
        cut = cuts(wide)[piece]
        block = y_ref.at[rep_at(-step * sign), :, cut]
        slot = 4 * route + step
        return remote(
            block, block, y_send.at[slot, piece], y_recv.at[slot, piece], {"rep": rep_at(sign)}
        )

    def y_landed(route, step, piece):
        sign = way if route == 0 else -way
        block = y_ref.at[rep_at(-(step + 1) * sign), :, cuts(wide)[piece]]
        slot = 4 * route + step
        return remote(
            block, block, y_send.at[slot, piece], y_recv.at[slot, piece], {"rep": rep_at(sign)}
        )

    y_ref[rep, :, 0:cols_a] = dot_nn(left_a, right_a)[0:rows]
    y_ref[rep, :, cols_a:width] = dot_nn(left_m, right_m)[0:rows]
    for piece in range(PIECES - 1):
        for route, _ in turns:
            y_copy(route, 0, piece).start()
    padded = left_a.shape[0]
    line = lax.broadcasted_iota(jnp.int32, (padded, cols_a), 0)
    column = lax.broadcasted_iota(jnp.int32, (padded, cols_a), 1)
    pick_a = jnp.where(column == me * rows + line, 1.0, 0.0).astype(jnp.float32)
    line = lax.broadcasted_iota(jnp.int32, (padded, cols_m), 0)
    column = lax.broadcasted_iota(jnp.int32, (padded, cols_m), 1)
    factors = [left_a, left_m, dot_nt(pick_a, right_a)]
    for group in range(4):
        start = (me - side * (shards // 2)) * (4 * rows) + group * rows
        pick_m = jnp.where(column == start + line, 1.0, 0.0).astype(jnp.float32)
        factors.append(dot_nt(pick_m, right_m))
    factors.append(jnp.zeros_like(left_a))
    for at, factor in enumerate(factors):
        lo = width + at * rank
        y_ref[rep, :, lo : lo + rank] = factor[0:rows]
    for route, _ in turns:
        y_copy(route, 0, PIECES - 1).start()

    for step in range(1, 4):
        for piece in range(PIECES):
            for route, steps in turns:
                if step < steps:
                    y_landed(route, step - 1, piece).wait_recv()
                    y_copy(route, step, piece).start()

    @pl.loop(1, reps)
    def _(step):
        small_copy(step, rep_at(step)).wait_recv()

    total = land_sm[0]
    for slot in range(1, reps):
        total = total + land_sm[slot]
    small_ref[...] = total

    @pl.loop(1, GROUP)
    def _(step):
        ba_first(step, flat).wait_send()
        ba_second(step, deep).wait_send()
        bm_second(step, deep).wait_send()

    @pl.when(in_side)
    def _():
        @pl.loop(1, GROUP)
        def _(step):
            bm_first(step, near).wait_send()

    @pl.loop(1, reps)
    def _(step):
        small_copy(step, rep).wait_send()

    for route, steps in turns:
        for piece in range(PIECES):
            y_landed(route, steps - 1, piece).wait_recv()
            for step in range(steps):
                x_copy(route, step, piece).wait_send()
                y_copy(route, step, piece).wait_send()


def power_call(shape, x, ba, bm, sg, roots):
    shards, reps, rows, cols_a, cols_m, rank, tiles = shape
    padded = 16
    width = cols_a + cols_m
    wide = width + 8 * rank
    share = tiles // GROUP
    assert shards == GROUP * GROUP and reps == GROUP and tiles % GROUP == 0
    f32 = jnp.float32
    vmem = pl.BlockSpec(memory_space=pltpu.VMEM)
    dma = pltpu.SemaphoreType.DMA

    def body(*refs):
        power_kernel(shape, *refs)

    return pl.pallas_call(
        body,
        out_shape=(
            jax.ShapeDtypeStruct((reps, rows, wide), f32),
            jax.ShapeDtypeStruct(sg.shape, f32),
        ),
        in_specs=[vmem] * 5,
        out_specs=(vmem, vmem),
        scratch_shapes=[
            pltpu.VMEM((7, rows, width), f32),
            pltpu.VMEM((7, rows, width), f32),
            pltpu.VMEM((padded, width), f32),
            pltpu.VMEM((GROUP, GROUP, rows, rank), f32),
            pltpu.VMEM((GROUP, 4, rows, 4 * rank), f32),
            pltpu.VMEM((shards // 2, 2 * rows, rank), f32),
            pltpu.VMEM((shards // 2, 4 * rows, rank), f32),
            pltpu.VMEM((reps,) + sg.shape, f32),
            pltpu.VMEM((2, padded, rank), f32),
            pltpu.VMEM((2, padded, rank), f32),
            pltpu.VMEM((2, GROUP, share, TILE, LANES), f32),
            pltpu.VMEM((2, GROUP, share, TILE, LANES), f32),
            pltpu.VMEM((2, share, TILE, LANES), f32),
            pltpu.VMEM((2, GROUP, share, TILE, LANES), f32),
            pltpu.VMEM((2, GROUP, share, TILE, LANES), f32),
            dma((7, PIECES)),
            dma((7, PIECES)),
            dma((7, PIECES)),
            dma((7, PIECES)),
            dma((reps,)),
            dma((reps,)),
            dma((2, GROUP)),
            dma((2, GROUP)),
            dma((2, GROUP)),
            dma((2, GROUP)),
            dma((2,)),
            dma((2,)),
            dma((2, GROUP)),
            dma((2, GROUP)),
            dma((2, GROUP)),
            dma((2, GROUP)),
            dma((2, GROUP)),
            dma((2, GROUP)),
        ],
        compiler_params=pltpu.CompilerParams(collective_id=0, has_side_effects=True),
        name="power_rounds",
    )(x, ba, bm, sg, roots)


def update(merged, approx, momentum, weights):
    error_out = (merged - approx)[None]
    momentum_out = momentum_decay * momentum + approx
    weights_out = weights - learn_rate * momentum_out
    return (error_out, momentum_out, weights_out)


def pick(array, index):
    return lax.dynamic_index_in_dim(array, index, 0, keepdims=False)


def per_device(
    attn_grad,
    attn_error,
    attn_basis,
    attn_roots,
    attn_momentum,
    attn_weights,
    mlp_grad,
    mlp_error,
    mlp_basis,
    mlp_roots,
    mlp_momentum,
    mlp_weights,
    small_grad,
    small_momentum,
    small_weights,
):
    shards, reps = lax.axis_size("shard"), lax.axis_size("rep")
    layers, kinds_a, rows, cols_a = attn_error.shape[1:]
    kinds_m, _, columns_m = mlp_error.shape[2:]
    rank = attn_basis.shape[-1]
    mats_a, mats_m = layers * kinds_a, layers * kinds_m
    cols_m = columns_m // 2
    assert mats_a == reps and 2 * mats_m == reps
    rep = lax.axis_index("rep")

    attn_merged = attn_grad[0].astype(jnp.float32) + attn_error[0]
    mlp_merged = mlp_grad[0].astype(jnp.float32) + mlp_error[0]
    x = jnp.concatenate(
        [
            attn_merged.reshape(mats_a, rows, cols_a),
            mlp_merged.reshape(mats_m, rows, 2, cols_m)
            .transpose(0, 2, 1, 3)
            .reshape(reps, rows, cols_m),
        ],
        axis=2,
    )
    ba = pick(attn_basis.reshape(mats_a, rows, rank), rep)
    bm = pick(mlp_basis.reshape(mats_m, 4, rows, rank), rep // 2)
    bm = bm.transpose(1, 0, 2).reshape(rows, 4 * rank)
    roots = jnp.stack(
        [
            pick(attn_roots.reshape(mats_a, 3, rank, rank), rep),
            pick(mlp_roots.reshape(mats_m, 3, rank, rank), rep // 2),
        ]
    )
    entries = small_grad.shape[1] * small_grad.shape[2]
    lines = -(-entries // LANES)
    sg = small_grad[0].astype(jnp.float32).reshape(entries)
    sg = jnp.pad(sg, (0, lines * LANES - entries)).reshape(lines, LANES)
    tiles = (cols_a + cols_m) * rank // (TILE * LANES)

    y, small = power_call((shards, reps, rows, cols_a, cols_m, rank, tiles), x, ba, bm, sg, roots)

    attn_approx = y[:, :, :cols_a].reshape(layers, kinds_a, rows, cols_a)
    mlp_approx = (
        y[:, :, cols_a : cols_a + cols_m]
        .reshape(mats_m, 2, rows, cols_m)
        .transpose(0, 2, 1, 3)
        .reshape(layers, kinds_m, rows, columns_m)
    )
    factors = y[:, :, cols_a + cols_m :].reshape(reps, rows, 8, rank)
    attn_left = factors[:, :, 0].reshape(layers, kinds_a, rows, rank)
    mlp_left = factors[0::2, :, 1].reshape(layers, kinds_m, rows, rank)
    attn_right = factors[:, :, 2].reshape(layers, kinds_a, rows, rank)
    mlp_right = factors[0::2, :, 3:7] + factors[1::2, :, 3:7]
    mlp_right = mlp_right.transpose(0, 2, 1, 3).reshape(layers, kinds_m, 4 * rows, rank)

    attn_error_out, attn_momentum_out, attn_weights_out = update(
        attn_merged, attn_approx, attn_momentum, attn_weights
    )
    mlp_error_out, mlp_momentum_out, mlp_weights_out = update(
        mlp_merged, mlp_approx, mlp_momentum, mlp_weights
    )
    small_total = small.reshape(lines * LANES)[:entries].reshape(small_momentum.shape)
    small_mean = small_total / float(reps)
    small_momentum_out = momentum_decay * small_momentum + small_mean
    small_weights_out = small_weights - learn_rate * small_momentum_out
    return (
        attn_error_out,
        mlp_error_out,
        attn_left,
        attn_right,
        mlp_left,
        mlp_right,
        attn_momentum_out,
        attn_weights_out,
        mlp_momentum_out,
        mlp_weights_out,
        small_momentum_out,
        small_weights_out,
    )


def solution(mesh):
    in_specs = (
        P("rep", None, None, "shard", None),
        P("rep", None, None, "shard", None),
        P(None, None, "shard", None),
        P(),
        P(None, None, "shard", None),
        P(None, None, "shard", None),
        P("rep", None, None, "shard", None),
        P("rep", None, None, "shard", None),
        P(None, None, "shard", None),
        P(),
        P(None, None, "shard", None),
        P(None, None, "shard", None),
        P("rep", None, "shard"),
        P(None, "shard"),
        P(None, "shard"),
    )
    out_specs = (
        P("rep", None, None, "shard", None),
        P("rep", None, None, "shard", None),
        P(None, None, "shard", None),
        P(None, None, "shard", None),
        P(None, None, "shard", None),
        P(None, None, "shard", None),
        P(None, None, "shard", None),
        P(None, None, "shard", None),
        P(None, None, "shard", None),
        P(None, None, "shard", None),
        P(None, "shard"),
        P(None, "shard"),
    )
    return jax.shard_map(
        per_device, mesh=mesh, in_specs=in_specs, out_specs=out_specs, check_vma=False
    )
```

time: 165 us -> 127 us (0.77)
  Pallas kernels: 141 us -> 102 us
    pallas_call x1, Pallas kernels: 141 us -> 102 us  [power_call(): pl.pallas_call(body, out_shape=(jax.ShapeDtypeStruct((reps, rows, wide),...]
where the time goes in v2:
time: 127 us; the launch traced here: 126 us
  Pallas kernels  102 us (80%)
  local copies, waits for them, and re-layouts  14.4 us (11%)
  other arithmetic  8.24 us (6%)
    pallas_call x1, Pallas kernels, power_call(): pl.pallas_call(body, out_shape=(jax.ShapeDtypeStruct((reps, rows, wide),...  102 us
    unnamed x28, local copies, waits for them, and re-layouts  7.61 us

profile of v2, /device:TPU:1, one launch (start us, length us, event | category | flops | bytes accessed | tf_op | source)
XLA Modules:
  0.0 125.7 jit_solution(5287871447801008605)
XLA Ops:
  0.6 0.0 copy-start.1
  0.7 0.0 copy-start.4
  0.7 0.8 convert_element_type.21
  1.5 0.6 bitcast_convert_fusion.refs_3_
  2.1 0.8 copy.56
  2.9 0.6 copy.89
  3.5 0.8 constant_dynamic-slice_fusion
  4.4 0.6 pad_maximum_fusion.1.refs_4_
  5.0 1.0 copy.57
  6.0 0.7 reshape.91.refs_2_
  6.7 1.0 convert_add_fusion
  7.7 0.1 copy.52
  7.8 0.0 copy-done.1
  7.8 0.0 copy-done.4
  7.8 0.3 copy_add_fusion
  8.2 0.7 add.46
  8.9 0.4 copy.55
  9.2 1.1 pad_maximum_fusion.refs_0_
  10.4 0.0 copy-start.7
  10.4 0.0 copy-start.8
  10.4 102.2 %power_rounds.1 = (f32[8,12,2560]{2,1,0:T(8,128)}, f32[3,128]{1,0:T(4,128)}) custom-call(f32[8,12,2304]{2,1,0:T(8,128)} %pad_maximum_fusion.refs_0_, f32[12,32]{1,0:T(8,128)} %bitcast.61, f32[12,128]{1,0:T(8,128)} %reshape.91.refs_2_, f32[3,128]{1,0:T(4,128)} %bitcast_convert_fusion.refs_3_, f32[2,3,32,32]{3,2,1,0:T(8,128)} %pad_maximum_fusion.1.refs_4_), custom_call_target="tpu_custom_call" | custom-call | tf_op jit(solution)/shard_map/power_rounds/pallas_call | solution.py:478
  112.5 0.0 copy-start
  112.6 0.8 slice_multiply_fusion
  113.3 0.1 div.22
  113.4 0.0 copy-done.7
  113.4 0.0 copy-done.8
  113.4 0.6 multiply_subtract_fusion.1
  114.0 0.9 slice.29
  114.9 0.1 copy.61
  115.0 0.1 reshape.99
  115.2 0.6 copy.69
  115.8 0.1 fusion.2
  115.9 0.6 copy.68
  116.5 0.6 copy.67
  117.2 0.7 copy.70
  117.9 0.0 copy-done
  117.9 0.1 slice.28
  118.0 0.5 copy.87
  118.5 0.9 copy_subtract_fusion.1
  119.4 0.7 reshape.102
  120.1 0.7 reshape.98
  120.8 0.0 copy-start.2
  120.9 0.0 copy-start.3
  120.9 0.3 sub.24
  121.2 0.9 copy.66
  122.0 0.0 copy-done.2
  122.0 0.0 copy-done.3
  122.1 0.7 copy_subtract_fusion
  122.8 0.0 copy-start.5
  122.8 0.0 copy-start.6
  122.8 0.9 copy.72
  123.7 0.9 copy.71
  124.5 0.0 copy-done.5
  124.5 0.0 copy-done.6
  124.5 1.2 multiply_subtract_fusion
  (7 shorter events, 0.2 us)
Async XLA Ops:
  0.6 7.2 %copy-start.1 = (f32[1,2,2,12,3072]{4,2,3,1,0:T(2,128)S(1)}, f32[1,2,2,12,3072]{4,2,3,1,0:T(2,128)}, u32[]{:S(2)}) copy-start(f32[1,2,2,12,3072]{4,2,3,1,0:T(2,128)} %param.22) | copy-start | bytes 1769476
  0.7 7.2 %copy-start.4 = (bf16[1,2,2,12,3072]{4,2,3,1,0:T(2,128)(2,1)S(1)}, bf16[1,2,2,12,3072]{4,2,3,1,0:T(2,128)(2,1)}, u32[]{:S(2)}) copy-start(bf16[1,2,2,12,3072]{4,2,3,1,0:T(2,128)(2,1)} %param.21) | copy-start | bytes 884740
  10.4 103.1 %copy-start.7 = (f32[2,156]{1,0:T(2,128)S(1)}, f32[2,156]{1,0:T(2,128)}, u32[]{:S(2)}) copy-start(f32[2,156]{1,0:T(2,128)} %param.29) | copy-start | bytes 3748
  10.4 103.1 %copy-start.8 = (f32[2,156]{1,0:T(2,128)S(1)}, f32[2,156]{1,0:T(2,128)}, u32[]{:S(2)}) copy-start(f32[2,156]{1,0:T(2,128)} %param.28) | copy-start | bytes 3748
  112.5 5.4 %copy-start = (f32[8,12,2560]{2,1,0:T(8,128)S(1)}, f32[8,12,2560]{2,1,0:T(8,128)}, u32[]{:S(2)}) copy-start(f32[8,12,2560]{2,1,0:T(8,128)} %get-tuple-element.14) | copy-start | bytes 2949124
  120.8 1.2 copy-start.2
  120.9 1.2 copy-start.3
  122.8 1.7 %copy-start.5 = (f32[2,4,12,768]{3,1,2,0:T(4,128)S(1)}, f32[2,4,12,768]{3,1,2,0:T(4,128)}, u32[]{:S(2)}) copy-start(f32[2,4,12,768]{3,1,2,0:T(4,128)} %param.20) | copy-start | bytes 884740
  122.8 1.7 %copy-start.6 = (f32[2,4,12,768]{3,1,2,0:T(4,128)S(1)}, f32[2,4,12,768]{3,1,2,0:T(4,128)}, u32[]{:S(2)}) copy-start(f32[2,4,12,768]{3,1,2,0:T(4,128)} %param.19) | copy-start | bytes 884740

commit v3 on v2

--- a/solution.py
+++ b/solution.py
@@ -38,13 +38,21 @@
 
 def power_kernel(
     shape,
+    ag_ref,
+    ae_ref,
+    mg_ref,
+    me_ref,
+    ab_ref,
+    mb_ref,
+    ar_ref,
+    mr_ref,
+    sgrad_ref,
+    y_ref,
+    small_ref,
     x_ref,
     ba_ref,
     bm_ref,
     sg_ref,
-    roots_ref,
-    y_ref,
-    small_ref,
     land_x,
     sum_x,
     s_ref,
@@ -128,6 +136,29 @@
         greet(flat_peer(step)[1])
         greet(deep_peer(step)[1])
 
+    layers, kinds_a, kinds_m = ag_ref.shape[0], ag_ref.shape[2], mg_ref.shape[2]
+    for layer in range(layers):
+        for row in range(rows):
+            lo = layer * kinds_a
+            value = ag_ref[layer, row].astype(jnp.float32) + ae_ref[layer, row]
+            x_ref[lo : lo + kinds_a, row, 0:cols_a] = value
+            value = mg_ref[layer, row].astype(jnp.float32) + me_ref[layer, row]
+            for kind in range(kinds_m):
+                for part_of in range(2):
+                    cut = slice(part_of * cols_m, (part_of + 1) * cols_m)
+                    at = (layer * kinds_m + kind) * 2 + part_of
+                    x_ref[at, row : row + 1, cols_a:width] = value[kind : kind + 1, cut]
+
+    spread = ab_ref[rep // kinds_a]
+    chosen = lax.broadcasted_iota(jnp.int32, spread.shape, 1) == lax.rem(rep, kinds_a)
+    ba_ref[...] = jnp.sum(jnp.where(chosen, spread, 0.0), axis=1)
+    own = rep // 2
+    upright = mb_ref[own // kinds_m, lax.rem(own, kinds_m)].T
+    for group in range(4):
+        bm_ref[:, group * rank : (group + 1) * rank] = upright[group * rows : (group + 1) * rows]
+    sg_ref[...] = jnp.zeros_like(sg_ref)
+    sg_ref[:, 0 : sgrad_ref.shape[1]] = sgrad_ref[...].astype(jnp.float32)
+
     pl.semaphore_wait(barrier, reps - 1 + 2 * (GROUP - 1))
 
     def cuts(total):
@@ -372,13 +403,13 @@
     first_m = dot_nn(s_ref[:, cols_a:width], basis_full_m)
     first_a = dot_nn(s_ref[:, 0:cols_a], basis_full_a)
     first_m = swapped(0, first_m)
-    lhat_a = dot_nn(first_a, roots_ref[0, 0])
-    lhat_m = dot_nn(first_m, roots_ref[1, 0])
+    lhat_a = dot_nn(first_a, ar_ref[rep, 0])
+    lhat_m = dot_nn(first_m, mr_ref[rep // 2, 0])
     one_a, one_m = right_round(0, lhat_a, lhat_m, 1.0)
     second_m = swapped(1, dot_nt(s_ref[:, cols_a:width], one_m))
     second_a = dot_nt(s_ref[:, 0:cols_a], one_a)
-    left_a = dot_nn(dot_nn(second_a, roots_ref[0, 1]), roots_ref[0, 2])
-    left_m = dot_nn(dot_nn(second_m, roots_ref[1, 1]), roots_ref[1, 2])
+    left_a = dot_nn(dot_nn(second_a, ar_ref[rep, 1]), ar_ref[rep, 2])
+    left_m = dot_nn(dot_nn(second_m, mr_ref[rep // 2, 1]), mr_ref[rep // 2, 2])
     right_a, right_m = right_round(1, left_a, left_m, 1.0 / reps)
 
     def y_copy(route, step, piece):
@@ -461,7 +492,7 @@
                 y_copy(route, step, piece).wait_send()
 
 
-def power_call(shape, x, ba, bm, sg, roots):
+def power_call(shape, *operands):
     shards, reps, rows, cols_a, cols_m, rank, tiles = shape
     padded = 16
     width = cols_a + cols_m
@@ -471,6 +502,8 @@
     f32 = jnp.float32
     vmem = pl.BlockSpec(memory_space=pltpu.VMEM)
     dma = pltpu.SemaphoreType.DMA
+    layers, entries = operands[-1].shape
+    small = (layers, -(-entries // LANES) * LANES)
 
     def body(*refs):
         power_kernel(shape, *refs)
@@ -479,11 +512,15 @@
         body,
         out_shape=(
             jax.ShapeDtypeStruct((reps, rows, wide), f32),
-            jax.ShapeDtypeStruct(sg.shape, f32),
+            jax.ShapeDtypeStruct(small, f32),
         ),
-        in_specs=[vmem] * 5,
+        in_specs=[vmem] * len(operands),
         out_specs=(vmem, vmem),
         scratch_shapes=[
+            pltpu.VMEM((reps, rows, width), f32),
+            pltpu.VMEM((rows, rank), f32),
+            pltpu.VMEM((rows, 4 * rank), f32),
+            pltpu.VMEM(small, f32),
             pltpu.VMEM((7, rows, width), f32),
             pltpu.VMEM((7, rows, width), f32),
             pltpu.VMEM((padded, width), f32),
@@ -491,7 +528,7 @@
             pltpu.VMEM((GROUP, 4, rows, 4 * rank), f32),
             pltpu.VMEM((shards // 2, 2 * rows, rank), f32),
             pltpu.VMEM((shards // 2, 4 * rows, rank), f32),
-            pltpu.VMEM((reps,) + sg.shape, f32),
+            pltpu.VMEM((reps,) + small, f32),
             pltpu.VMEM((2, padded, rank), f32),
             pltpu.VMEM((2, padded, rank), f32),
             pltpu.VMEM((2, GROUP, share, TILE, LANES), f32),
@@ -499,39 +536,138 @@
             pltpu.VMEM((2, share, TILE, LANES), f32),
             pltpu.VMEM((2, GROUP, share, TILE, LANES), f32),
             pltpu.VMEM((2, GROUP, share, TILE, LANES), f32),
-            dma((7, PIECES)),
-            dma((7, PIECES)),
-            dma((7, PIECES)),
-            dma((7, PIECES)),
-            dma((reps,)),
-            dma((reps,)),
-            dma((2, GROUP)),
-            dma((2, GROUP)),
-            dma((2, GROUP)),
-            dma((2, GROUP)),
-            dma((2,)),
-            dma((2,)),
-            dma((2, GROUP)),
-            dma((2, GROUP)),
-            dma((2, GROUP)),
-            dma((2, GROUP)),
-            dma((2, GROUP)),
-            dma((2, GROUP)),
-        ],
+        ]
+        + [dma((7, PIECES))] * 4
+        + [dma((reps,))] * 2
+        + [dma((2, GROUP))] * 4
+        + [dma((2,))] * 2
+        + [dma((2, GROUP))] * 6,
         compiler_params=pltpu.CompilerParams(collective_id=0, has_side_effects=True),
         name="power_rounds",
-    )(x, ba, bm, sg, roots)
-
-
-def update(merged, approx, momentum, weights):
-    error_out = (merged - approx)[None]
-    momentum_out = momentum_decay * momentum + approx
-    weights_out = weights - learn_rate * momentum_out
-    return (error_out, momentum_out, weights_out)
-
-
-def pick(array, index):
-    return lax.dynamic_index_in_dim(array, index, 0, keepdims=False)
+    )(*operands)
+
+
+def update_kernel(
+    shape,
+    y_ref,
+    small_ref,
+    ag_ref,
+    ae_ref,
+    am_ref,
+    aw_ref,
+    mg_ref,
+    me_ref,
+    mm_ref,
+    mw_ref,
+    sm_ref,
+    sw_ref,
+    ae_out,
+    me_out,
+    al_out,
+    ar_out,
+    ml_out,
+    mr_out,
+    am_out,
+    aw_out,
+    mm_out,
+    mw_out,
+    sm_out,
+    sw_out,
+    turned,
+):
+    shards, reps, rows, cols_a, cols_m, rank, tiles = shape
+    width = cols_a + cols_m
+    layers, kinds_a, kinds_m = ag_ref.shape[0], ag_ref.shape[2], mg_ref.shape[2]
+
+    def finish(grad, error, momentum, weights, approx):
+        stepped = momentum_decay * momentum + approx
+        return (
+            grad.astype(jnp.float32) + error - approx,
+            stepped,
+            weights - learn_rate * stepped,
+        )
+
+    def lanes(at):
+        return slice(width + at * rank, width + (at + 1) * rank)
+
+    for layer in range(layers):
+        for row in range(rows):
+            lo = layer * kinds_a
+            approx = y_ref[lo : lo + kinds_a, row, 0:cols_a]
+            ae_out[layer, row], am_out[layer, row], aw_out[layer, row] = finish(
+                ag_ref[layer, row],
+                ae_ref[layer, row],
+                am_ref[layer, row],
+                aw_ref[layer, row],
+                approx,
+            )
+            al_out[layer, row] = y_ref[lo : lo + kinds_a, row, lanes(0)]
+            ar_out[layer, row] = y_ref[lo : lo + kinds_a, row, lanes(2)]
+            first = [(layer * kinds_m + kind) * 2 for kind in range(kinds_m)]
+            approx = jnp.concatenate(
+                [
+                    jnp.concatenate(
+                        [y_ref[at, row : row + 1, cols_a:width] for at in (one, one + 1)], axis=1
+                    )
+                    for one in first
+                ],
+                axis=0,
+            )
+            me_out[layer, row], mm_out[layer, row], mw_out[layer, row] = finish(
+                mg_ref[layer, row],
+                me_ref[layer, row],
+                mm_ref[layer, row],
+                mw_ref[layer, row],
+                approx,
+            )
+            for kind in range(kinds_m):
+                ml_out[layer, row, kind : kind + 1] = y_ref[first[kind], row : row + 1, lanes(1)]
+        for kind in range(kinds_m):
+            one = (layer * kinds_m + kind) * 2
+            for group in range(4):
+                turned[group * rows : (group + 1) * rows] = (
+                    y_ref[one, :, lanes(3 + group)] + y_ref[one + 1, :, lanes(3 + group)]
+                )
+            mr_out[layer, kind] = turned[...].T
+    entries = sm_ref.shape[1]
+    mean = small_ref[:, 0:entries] / float(reps)
+    stepped = momentum_decay * sm_ref[...] + mean
+    sm_out[...] = stepped
+    sw_out[...] = sw_ref[...] - learn_rate * stepped
+
+
+def update_call(shape, *operands):
+    shards, reps, rows, cols_a, cols_m, rank, tiles = shape
+    f32 = jnp.float32
+    attn, mlp, small = operands[3].shape, operands[7].shape, operands[-1].shape
+    layers, kinds_a, kinds_m = attn[0], attn[2], mlp[2]
+    vmem = pl.BlockSpec(memory_space=pltpu.VMEM)
+
+    def body(*refs):
+        update_kernel(shape, *refs)
+
+    shapes = [
+        attn,
+        mlp,
+        (layers, rows, kinds_a, rank),
+        (layers, rows, kinds_a, rank),
+        (layers, rows, kinds_m, rank),
+        (layers, kinds_m, rank, 4 * rows),
+        attn,
+        attn,
+        mlp,
+        mlp,
+        small,
+        small,
+    ]
+    return pl.pallas_call(
+        body,
+        out_shape=tuple(jax.ShapeDtypeStruct(each, f32) for each in shapes),
+        in_specs=[vmem] * len(operands),
+        out_specs=(vmem,) * len(shapes),
+        scratch_shapes=[pltpu.VMEM((4 * rows, rank), f32)],
+        name="apply_update",
+    )(*operands)
 
 
 def per_device(
@@ -558,73 +694,54 @@
     mats_a, mats_m = layers * kinds_a, layers * kinds_m
     cols_m = columns_m // 2
     assert mats_a == reps and 2 * mats_m == reps
-    rep = lax.axis_index("rep")
-
-    attn_merged = attn_grad[0].astype(jnp.float32) + attn_error[0]
-    mlp_merged = mlp_grad[0].astype(jnp.float32) + mlp_error[0]
-    x = jnp.concatenate(
-        [
-            attn_merged.reshape(mats_a, rows, cols_a),
-            mlp_merged.reshape(mats_m, rows, 2, cols_m)
-            .transpose(0, 2, 1, 3)
-            .reshape(reps, rows, cols_m),
-        ],
-        axis=2,
-    )
-    ba = pick(attn_basis.reshape(mats_a, rows, rank), rep)
-    bm = pick(mlp_basis.reshape(mats_m, 4, rows, rank), rep // 2)
-    bm = bm.transpose(1, 0, 2).reshape(rows, 4 * rank)
-    roots = jnp.stack(
-        [
-            pick(attn_roots.reshape(mats_a, 3, rank, rank), rep),
-            pick(mlp_roots.reshape(mats_m, 3, rank, rank), rep // 2),
-        ]
-    )
-    entries = small_grad.shape[1] * small_grad.shape[2]
-    lines = -(-entries // LANES)
-    sg = small_grad[0].astype(jnp.float32).reshape(entries)
-    sg = jnp.pad(sg, (0, lines * LANES - entries)).reshape(lines, LANES)
     tiles = (cols_a + cols_m) * rank // (TILE * LANES)
-
-    y, small = power_call((shards, reps, rows, cols_a, cols_m, rank, tiles), x, ba, bm, sg, roots)
-
-    attn_approx = y[:, :, :cols_a].reshape(layers, kinds_a, rows, cols_a)
-    mlp_approx = (
-        y[:, :, cols_a : cols_a + cols_m]
-        .reshape(mats_m, 2, rows, cols_m)
-        .transpose(0, 2, 1, 3)
-        .reshape(layers, kinds_m, rows, columns_m)
-    )
-    factors = y[:, :, cols_a + cols_m :].reshape(reps, rows, 8, rank)
-    attn_left = factors[:, :, 0].reshape(layers, kinds_a, rows, rank)
-    mlp_left = factors[0::2, :, 1].reshape(layers, kinds_m, rows, rank)
-    attn_right = factors[:, :, 2].reshape(layers, kinds_a, rows, rank)
-    mlp_right = factors[0::2, :, 3:7] + factors[1::2, :, 3:7]
-    mlp_right = mlp_right.transpose(0, 2, 1, 3).reshape(layers, kinds_m, 4 * rows, rank)
-
-    attn_error_out, attn_momentum_out, attn_weights_out = update(
-        attn_merged, attn_approx, attn_momentum, attn_weights
-    )
-    mlp_error_out, mlp_momentum_out, mlp_weights_out = update(
-        mlp_merged, mlp_approx, mlp_momentum, mlp_weights
-    )
-    small_total = small.reshape(lines * LANES)[:entries].reshape(small_momentum.shape)
-    small_mean = small_total / float(reps)
-    small_momentum_out = momentum_decay * small_momentum + small_mean
-    small_weights_out = small_weights - learn_rate * small_momentum_out
+    shape = (shards, reps, rows, cols_a, cols_m, rank, tiles)
+
+    def flip(array):
+        return array.transpose(0, 2, 1, 3)
+
+    ag, ae = flip(attn_grad[0]), flip(attn_error[0])
+    mg, me = flip(mlp_grad[0]), flip(mlp_error[0])
+    y, small = power_call(
+        shape,
+        ag,
+        ae,
+        mg,
+        me,
+        flip(attn_basis),
+        mlp_basis.transpose(0, 1, 3, 2),
+        attn_roots.reshape(mats_a, 3, rank, rank),
+        mlp_roots.reshape(mats_m, 3, rank, rank),
+        small_grad[0],
+    )
+    outs = update_call(
+        shape,
+        y,
+        small,
+        ag,
+        ae,
+        flip(attn_momentum),
+        flip(attn_weights),
+        mg,
+        me,
+        flip(mlp_momentum),
+        flip(mlp_weights),
+        small_momentum,
+        small_weights,
+    )
     return (
-        attn_error_out,
-        mlp_error_out,
-        attn_left,
-        attn_right,
-        mlp_left,
-        mlp_right,
-        attn_momentum_out,
-        attn_weights_out,
-        mlp_momentum_out,
-        mlp_weights_out,
-        small_momentum_out,
-        small_weights_out,
+        flip(outs[0])[None],
+        flip(outs[1])[None],
+        flip(outs[2]),
+        flip(outs[3]),
+        flip(outs[4]),
+        outs[5].transpose(0, 1, 3, 2),
+        flip(outs[6]),
+        flip(outs[7]),
+        flip(outs[8]),
+        flip(outs[9]),
+        outs[10],
+        outs[11],
     )
 
 

time: 127 us -> 108 us (0.85)
  local copies, waits for them, and re-layouts: 14.4 us -> 0 us
  other arithmetic: 8.24 us -> 0 us
  Pallas kernels: 102 us -> 107 us
    unnamed x28 -> x0, local copies, waits for them, and re-layouts: 7.61 us -> none
    pallas_call x0 -> x1, Pallas kernels: none -> 4.35 us  [update_call(): pl.pallas_call(body, out_shape=tuple((jax.ShapeDtypeStruct(each, f32) for...]
    sub x5 -> x0, other arithmetic: 3.71 us -> none  [the longest x2 1.88 us: update(): weights_out = weights - learn_rate * momentum_out]
    reshape x5 -> x0, local copies, waits for them, and re-layouts: 2.68 us -> none  [the longest x3 1.88 us: per_device(): mlp_approx = y[:, :, cols_a:cols_a + cols_m].reshape(mats_m, 2, rows, col...]
    add x2 -> x0, other arithmetic: 1.37 us -> none  [the longest x1 1.02 us: per_device(): attn_merged = attn_grad[0].astype(jnp.float32) + attn_error[0]]
where the time goes in v3:
time: 108 us; the launch traced here: 107 us
  Pallas kernels  107 us (99%)
    pallas_call x1, Pallas kernels, power_call(): pl.pallas_call(body, out_shape=(jax.ShapeDtypeStruct((reps, rows, wide),...  102 us
    pallas_call x1, Pallas kernels, update_call(): pl.pallas_call(body, out_shape=tuple((jax.ShapeDtypeStruct(each, f32) for...  4.35 us

profile of v3, /device:TPU:1, one launch (start us, length us, event | category | flops | bytes accessed | tf_op | source)
XLA Modules:
  0.0 107.2 jit_solution(13533199470467025303)
XLA Ops:
  0.6 102.2 %power_rounds.1 = (f32[8,12,2560]{2,1,0:T(8,128)}, f32[2,256]{1,0:T(2,128)}) custom-call(bf16[2,12,4,768]{3,2,1,0:T(4,128)(2,1)} %bitcast.43, f32[2,12,4,768]{3,2,1,0:T(4,128)} %bitcast.37, bf16[2,12,2,3072]{3,2,1,0:T(2,128)(2,1)} %bitcast.39, f32[2,12,2,3072]{3,2,1,0:T(2,128)} %bitcast.35, f32[2,12,4,32]{3,2,1,0:T(4,128)} %bitcast.50, ...), custom_call_target="tpu_custom_call" | custom-call | tf_op jit(solution)/shard_map/power_rounds/pallas_call | solution.py:511
  102.9 4.4 %apply_update.1 = (f32[2,12,4,768]{3,2,1,0:T(4,128)}, f32[2,12,2,3072]{3,2,1,0:T(2,128)}, f32[2,12,4,32]{3,2,1,0:T(4,128)}, f32[2,12,4,32]{3,2,1,0:T(4,128)}, f3...) custom-call(f32[8,12,2560]{2,1,0:T(8,128)} %get-tuple-element.26.ref, ...), custom_call_target="tpu_custom_call" | custom-call | tf_op jit(solution)/shard_map/apply_update/pallas_call | solution.py:663

commit v4 on v3

--- a/solution.py
+++ b/solution.py
@@ -293,129 +293,167 @@
             x_copy(route, steps - 1, piece).wait_recv()
         s_ref[0:rows, cut] = x_ref[rep, :, cut] + (land_x[3, :, cut] + land_x[6, :, cut])
 
-    def swapped(turn, term):
-        swap_out[turn] = term
-        copy = remote(
+    def swap(turn):
+        return remote(
             swap_out.at[turn],
             swap_in.at[turn],
             swap_send.at[turn],
             swap_recv.at[turn],
             {"rep": pair},
         )
-        copy.start()
-        copy.wait()
+
+    def swap_begin(turn, term):
+        swap_out[turn] = term
+        swap(turn).start()
+
+    def swap_end(turn, term):
+        swap(turn).wait()
         return term + swap_in[turn]
 
-    share = tiles // GROUP
-    blocks_a, blocks = cols_a // LANES, width // LANES
+    share = tiles // GROUP // PIECES
+    span = width // PIECES
+    blocks = span // LANES
     high = rank // TILE
 
-    def right_round(turn, left_a, left_m, scale):
-        right_a = dot_tn(left_a, s_ref[:, 0:cols_a])
-        right_m = dot_tn(left_m, s_ref[:, cols_a:width])
-        for block in range(blocks):
-            value, at = (right_a, block) if block < blocks_a else (right_m, block - blocks_a)
-            for line in range(high):
-                tile = block * high + line
-                part[turn, tile // share, tile % share] = value[
-                    line * TILE : (line + 1) * TILE, at * LANES : (at + 1) * LANES
-                ]
-
-        def p_copy(step, slot):
+    def columns(piece):
+        return slice(piece * span, (piece + 1) * span)
+
+    def right_round(turn, left_of, scale, use):
+        def p_copy(piece, step, slot):
             to, where = flat_peer(step)
             return remote(
-                part.at[turn, to],
-                land_p.at[turn, slot],
-                p_send.at[turn, step],
-                p_recv.at[turn, slot],
+                part.at[turn, piece, to],
+                land_p.at[turn, piece, slot],
+                p_send.at[turn * PIECES + piece, step],
+                p_recv.at[turn * PIECES + piece, slot],
                 where,
             )
 
-        def z_copy(step, slot):
+        def z_copy(piece, step, slot):
             to, where = deep_peer(step)
             return remote(
-                part_z.at[turn],
-                land_z.at[turn, slot],
-                z_send.at[turn, step],
-                z_recv.at[turn, slot],
+                part_z.at[turn, piece],
+                land_z.at[turn, piece, slot],
+                z_send.at[turn * PIECES + piece, step],
+                z_recv.at[turn * PIECES + piece, slot],
                 where,
             )
 
-        def g_copy(step, slot):
+        def g_copy(piece, step, slot):
             to, where = flat_peer(step)
             return remote(
-                full.at[turn, slot],
-                full.at[turn, slot],
-                g_send.at[turn, step],
-                g_recv.at[turn, slot],
+                full.at[turn, piece, slot],
+                full.at[turn, piece, slot],
+                g_send.at[turn * PIECES + piece, step],
+                g_recv.at[turn * PIECES + piece, slot],
                 where,
             )
 
-        @pl.loop(1, GROUP)
-        def _(step):
-            p_copy(step, flat).start()
-
-        land_p[turn, flat] = part[turn, flat]
-
-        @pl.loop(1, GROUP)
-        def _(step):
-            p_copy(step, flat_peer(step)[0]).wait_recv()
-
-        part_z[turn] = jnp.sum(land_p[turn], axis=0)
-
-        @pl.loop(1, GROUP)
-        def _(step):
-            z_copy(step, deep).start()
-
-        land_z[turn, deep] = part_z[turn]
-
-        @pl.loop(1, GROUP)
-        def _(step):
-            z_copy(step, deep_peer(step)[0]).wait_recv()
-
-        full[turn, flat] = jnp.sum(land_z[turn], axis=0) * scale
-
-        @pl.loop(1, GROUP)
-        def _(step):
-            g_copy(step, flat).start()
-
-        @pl.loop(1, GROUP)
-        def _(step):
-            g_copy(step, flat_peer(step)[0]).wait_recv()
-
-        @pl.loop(1, GROUP)
-        def _(step):
-            p_copy(step, flat).wait_send()
-            z_copy(step, deep).wait_send()
-            g_copy(step, flat).wait_send()
-
-        whole = full[turn].reshape(tiles, TILE, LANES)
-        pieces = [
-            whole[block * high : (block + 1) * high].reshape(rank, LANES) for block in range(blocks)
-        ]
-        return (
-            jnp.concatenate(pieces[:blocks_a], axis=1),
-            jnp.concatenate(pieces[blocks_a:], axis=1),
-        )
+        for piece in range(PIECES):
+            value = dot_tn(left_of(piece), s_ref[:, columns(piece)])
+            for block in range(blocks):
+                for line in range(high):
+                    tile = block * high + line
+                    part[turn, piece, tile // share, tile % share] = value[
+                        line * TILE : (line + 1) * TILE, block * LANES : (block + 1) * LANES
+                    ]
+
+            @pl.loop(1, GROUP)
+            def _(step):
+                p_copy(piece, step, flat).start()
+
+            land_p[turn, piece, flat] = part[turn, piece, flat]
+
+        for piece in range(PIECES):
+
+            @pl.loop(1, GROUP)
+            def _(step):
+                p_copy(piece, step, flat_peer(step)[0]).wait_recv()
+
+            part_z[turn, piece] = jnp.sum(land_p[turn, piece], axis=0)
+
+            @pl.loop(1, GROUP)
+            def _(step):
+                z_copy(piece, step, deep).start()
+
+            land_z[turn, piece, deep] = part_z[turn, piece]
+
+        for piece in range(PIECES):
+
+            @pl.loop(1, GROUP)
+            def _(step):
+                z_copy(piece, step, deep_peer(step)[0]).wait_recv()
+
+            full[turn, piece, flat] = jnp.sum(land_z[turn, piece], axis=0) * scale
+
+            @pl.loop(1, GROUP)
+            def _(step):
+                g_copy(piece, step, flat).start()
+
+        for piece in range(PIECES):
+
+            @pl.loop(1, GROUP)
+            def _(step):
+                g_copy(piece, step, flat_peer(step)[0]).wait_recv()
+
+            whole = full[turn, piece].reshape(tiles // PIECES, TILE, LANES)
+            use(
+                piece,
+                jnp.concatenate(
+                    [
+                        whole[block * high : (block + 1) * high].reshape(rank, LANES)
+                        for block in range(blocks)
+                    ],
+                    axis=1,
+                ),
+            )
+
+        for piece in range(PIECES):
+
+            @pl.loop(1, GROUP)
+            def _(step):
+                p_copy(piece, step, flat).wait_send()
+                z_copy(piece, step, deep).wait_send()
+                g_copy(piece, step, flat).wait_send()
+
+    def once(make_a, make_m):
+        held = []
+
+        def left_of(piece):
+            if piece == 0:
+                held.append(make_a())
+            elif piece == 1:
+                held.append(make_m())
+            return held[min(piece, 1)]
+
+        return held, left_of
 
     basis_full_a = basis_a[...].reshape(cols_a, rank)
     basis_full_m = basis_m[...].reshape(cols_m, rank)
     first_m = dot_nn(s_ref[:, cols_a:width], basis_full_m)
-    first_a = dot_nn(s_ref[:, 0:cols_a], basis_full_a)
-    first_m = swapped(0, first_m)
-    lhat_a = dot_nn(first_a, ar_ref[rep, 0])
-    lhat_m = dot_nn(first_m, mr_ref[rep // 2, 0])
-    one_a, one_m = right_round(0, lhat_a, lhat_m, 1.0)
-    second_m = swapped(1, dot_nt(s_ref[:, cols_a:width], one_m))
-    second_a = dot_nt(s_ref[:, 0:cols_a], one_a)
-    left_a = dot_nn(dot_nn(second_a, ar_ref[rep, 1]), ar_ref[rep, 2])
-    left_m = dot_nn(dot_nn(second_m, mr_ref[rep // 2, 1]), mr_ref[rep // 2, 2])
-    right_a, right_m = right_round(1, left_a, left_m, 1.0 / reps)
+    swap_begin(0, first_m)
+
+    seconds = []
+    right_round(
+        0,
+        once(
+            lambda: dot_nn(dot_nn(s_ref[:, 0:cols_a], basis_full_a), ar_ref[rep, 0]),
+            lambda: dot_nn(swap_end(0, first_m), mr_ref[rep // 2, 0]),
+        )[1],
+        1.0,
+        lambda piece, right: seconds.append(dot_nt(s_ref[:, columns(piece)], right)),
+    )
+    second_m = seconds[1] + seconds[2]
+    swap_begin(1, second_m)
+
+    y_edges = [0, span, 2 * span, wide]
+
+    def y_cut(piece):
+        return slice(y_edges[piece], y_edges[piece + 1])
 
     def y_copy(route, step, piece):
         sign = way if route == 0 else -way
-        cut = cuts(wide)[piece]
-        block = y_ref.at[rep_at(-step * sign), :, cut]
+        block = y_ref.at[rep_at(-step * sign), :, y_cut(piece)]
         slot = 4 * route + step
         return remote(
             block, block, y_send.at[slot, piece], y_recv.at[slot, piece], {"rep": rep_at(sign)}
@@ -423,17 +461,30 @@
 
     def y_landed(route, step, piece):
         sign = way if route == 0 else -way
-        block = y_ref.at[rep_at(-(step + 1) * sign), :, cuts(wide)[piece]]
+        block = y_ref.at[rep_at(-(step + 1) * sign), :, y_cut(piece)]
         slot = 4 * route + step
         return remote(
             block, block, y_send.at[slot, piece], y_recv.at[slot, piece], {"rep": rep_at(sign)}
         )
 
-    y_ref[rep, :, 0:cols_a] = dot_nn(left_a, right_a)[0:rows]
-    y_ref[rep, :, cols_a:width] = dot_nn(left_m, right_m)[0:rows]
-    for piece in range(PIECES - 1):
-        for route, _ in turns:
-            y_copy(route, 0, piece).start()
+    rights = []
+    lefts, left_of = once(
+        lambda: dot_nn(dot_nn(seconds[0], ar_ref[rep, 1]), ar_ref[rep, 2]),
+        lambda: dot_nn(
+            dot_nn(swap_end(1, second_m), mr_ref[rep // 2, 1]), mr_ref[rep // 2, 2]
+        ),
+    )
+
+    def send_approx(piece, right):
+        rights.append(right)
+        y_ref[rep, :, columns(piece)] = dot_nn(lefts[min(piece, 1)], right)[0:rows]
+        if piece < PIECES - 1:
+            for route, _ in turns:
+                y_copy(route, 0, piece).start()
+
+    right_round(1, left_of, 1.0 / reps, send_approx)
+    left_a, left_m = lefts
+    right_a, right_m = rights[0], jnp.concatenate(rights[1:], axis=1)
     padded = left_a.shape[0]
     line = lax.broadcasted_iota(jnp.int32, (padded, cols_a), 0)
     column = lax.broadcasted_iota(jnp.int32, (padded, cols_a), 1)
@@ -497,8 +548,9 @@
     padded = 16
     width = cols_a + cols_m
     wide = width + 8 * rank
-    share = tiles // GROUP
-    assert shards == GROUP * GROUP and reps == GROUP and tiles % GROUP == 0
+    share = tiles // GROUP // PIECES
+    assert shards == GROUP * GROUP and reps == GROUP
+    assert tiles == share * GROUP * PIECES and width == PIECES * cols_a
     f32 = jnp.float32
     vmem = pl.BlockSpec(memory_space=pltpu.VMEM)
     dma = pltpu.SemaphoreType.DMA
@@ -531,17 +583,17 @@
             pltpu.VMEM((reps,) + small, f32),
             pltpu.VMEM((2, padded, rank), f32),
             pltpu.VMEM((2, padded, rank), f32),
-            pltpu.VMEM((2, GROUP, share, TILE, LANES), f32),
-            pltpu.VMEM((2, GROUP, share, TILE, LANES), f32),
-            pltpu.VMEM((2, share, TILE, LANES), f32),
-            pltpu.VMEM((2, GROUP, share, TILE, LANES), f32),
-            pltpu.VMEM((2, GROUP, share, TILE, LANES), f32),
+            pltpu.VMEM((2, PIECES, GROUP, share, TILE, LANES), f32),
+            pltpu.VMEM((2, PIECES, GROUP, share, TILE, LANES), f32),
+            pltpu.VMEM((2, PIECES, share, TILE, LANES), f32),
+            pltpu.VMEM((2, PIECES, GROUP, share, TILE, LANES), f32),
+            pltpu.VMEM((2, PIECES, GROUP, share, TILE, LANES), f32),
         ]
         + [dma((7, PIECES))] * 4
         + [dma((reps,))] * 2
         + [dma((2, GROUP))] * 4
         + [dma((2,))] * 2
-        + [dma((2, GROUP))] * 6,
+        + [dma((2 * PIECES, GROUP))] * 6,
         compiler_params=pltpu.CompilerParams(collective_id=0, has_side_effects=True),
         name="power_rounds",
     )(*operands)

time: 108 us -> 99.9 us (0.925)
  Pallas kernels: 107 us -> 99 us
    pallas_call x1, Pallas kernels: 102 us -> 94.7 us  [power_call(): pl.pallas_call(body, out_shape=(jax.ShapeDtypeStruct((reps, rows, wide),...]
where the time goes in v4:
time: 99.9 us; the launch traced here: 99.7 us
  Pallas kernels  99 us (99%)
    pallas_call x1, Pallas kernels, power_call(): pl.pallas_call(body, out_shape=(jax.ShapeDtypeStruct((reps, rows, wide),...  94.7 us
    pallas_call x1, Pallas kernels, update_call(): pl.pallas_call(body, out_shape=tuple((jax.ShapeDtypeStruct(each, f32) for...  4.35 us

profile of v4, /device:TPU:1, one launch (start us, length us, event | category | flops | bytes accessed | tf_op | source)
XLA Modules:
  0.0 99.7 jit_solution(728547169825681600)
XLA Ops:
  0.6 94.7 %power_rounds.1 = (f32[8,12,2560]{2,1,0:T(8,128)}, f32[2,256]{1,0:T(2,128)}) custom-call(bf16[2,12,4,768]{3,2,1,0:T(4,128)(2,1)} %bitcast.43, f32[2,12,4,768]{3,2,1,0:T(4,128)} %bitcast.37, bf16[2,12,2,3072]{3,2,1,0:T(2,128)(2,1)} %bitcast.39, f32[2,12,2,3072]{3,2,1,0:T(2,128)} %bitcast.35, f32[2,12,4,32]{3,2,1,0:T(4,128)} %bitcast.50, ...), custom_call_target="tpu_custom_call" | custom-call | tf_op jit(solution)/shard_map/power_rounds/pallas_call | solution.py:563
  95.3 4.4 %apply_update.1 = (f32[2,12,4,768]{3,2,1,0:T(4,128)}, f32[2,12,2,3072]{3,2,1,0:T(2,128)}, f32[2,12,4,32]{3,2,1,0:T(4,128)}, f32[2,12,4,32]{3,2,1,0:T(4,128)}, f3...) custom-call(f32[8,12,2560]{2,1,0:T(8,128)} %get-tuple-element.26.ref, ...), custom_call_target="tpu_custom_call" | custom-call | tf_op jit(solution)/shard_map/apply_update/pallas_call | solution.py:715
